TPU v7x, 256 devices: a whole 4x4x8 slice. The times are simulated.
256 devices in a mesh: sub: 64 (over x, z, core), blk: 4 (over y).
Axes of the slice: x: 4, y: 4, z: 8, core: 2. Of those that a mesh axis runs over, the one named last changes fastest.
Arguments:
- residual: float32 [64, 8, 375, 256], P('sub', 'blk'), may hold values from -6 to 6
- stiffness: bfloat16 [64, 8, 16, 375, 375], P('sub', 'blk'), may hold values from -0.078125 to 0.078125
- pattern: int32 [64, 8, 16], P('sub', 'blk'), may hold values from 0 to 7
- neumann_inv: bfloat16 [64, 8, 375, 375], P('sub', 'blk'), may hold values from -0.3125 to 0.3125
- dirichlet_inv: bfloat16 [64, 8, 375, 375], P('sub', 'blk'), may hold values from -0.3125 to 0.3125
- basis: bfloat16 [64, 8, 375, 192], P('sub', 'blk'), may hold values from -0.5 to 0.5
- node_ops: float32 [64, 6, 192, 192], P('sub'), as said below
- root_inv: float32 [192, 192], replicated, may hold values from -0.4375 to 0.4375
Outputs:
- preconditioned: float32 [64, 8, 375, 256], P('sub', 'blk')
Inputs may be any that keep to these rules, and one draw needn't show every extreme that they name: node_ops[s, l] equals node_ops[t, l] whenever s // 2**l == t // 2**l: one map for each tree node, held by all of its subdomains.
All inputs are finite; a program needn't handle non-finite values.
Results may differ from a plain program's by a relative error of at most 0.004.
Values may be sent and summed in bfloat16 or wider, within the bound.
A program may use at most 64 MiB of HBM per device.

v0:
```python
import jax
import jax.numpy as jnp
from jax import lax
from jax.sharding import PartitionSpec as P


def swapped(x, axis, distance):
    return lax.ppermute(x, axis, [(i, i ^ 1 << distance) for i in range(lax.axis_size(axis))])


def passed_along(x, axis, by):
    count = lax.axis_size(axis)
    pairs = [(i, i + by) for i in range(count) if 0 <= i + by < count]
    return lax.ppermute(x, axis, pairs)


def tree_solve(values, maps, root_inv):
    highest = lax.Precision.HIGHEST
    level_values = [values]
    current = values
    for level in range(maps.shape[0]):
        own = jnp.einsum("mk,mr->kr", maps[level], current, precision=highest)
        current = own + swapped(own, "sub", level)
        level_values.append(current)
    field = jnp.dot(root_inv, current, precision=highest)
    for level in reversed(range(maps.shape[0])):
        field = jnp.dot(maps[level], field, precision=highest) + level_values[level]
    return field


def shards(residual, stiffness, pattern, neumann_inv, dirichlet_inv, basis, node_ops, root_inv):
    subs = lax.axis_size("sub")
    here = lax.axis_index("sub")
    per_device = residual.shape[1]
    local_ids = jnp.arange(per_device)
    shared = (local_ids == 0) & (here > 0) | (local_ids == per_device - 1) & (here < subs - 1)
    scale = jnp.where(shared, 0.5, 1.0).astype(jnp.float32)[:, None, None]
    scaled_bf = (residual[0] * scale).astype(jnp.bfloat16)
    local_fix = jnp.einsum(
        "jab,jbr->jar", neumann_inv[0], scaled_bf, preferred_element_type=jnp.float32
    )
    partial_coarse = jnp.einsum(
        "jbm,jbr->mr", basis[0], scaled_bf, preferred_element_type=jnp.float32
    )
    total = lax.psum(partial_coarse, "blk")
    coarse_fix = tree_solve(total, node_ops[0], root_inv).astype(jnp.bfloat16)
    fix_term = jnp.einsum("jbm,mr->jbr", basis[0], coarse_fix, preferred_element_type=jnp.float32)
    combined = ((local_fix + fix_term) * scale)[None]
    incoming = passed_along(combined[:, -1], "sub", 1)
    first = combined[:, 0] + incoming
    returned = passed_along(first, "sub", -1)
    last = jnp.where(here < subs - 1, returned, combined[:, -1])
    assembled = jnp.concatenate([first[:, None], combined[:, 1:-1], last[:, None]], axis=1)
    assembled_bf = assembled.astype(jnp.bfloat16)
    gathered = lax.all_gather(assembled_bf, "blk", axis=1, tiled=True)
    picked = jnp.take(gathered[0], pattern[0], axis=0)
    coupled = jnp.einsum("jpab,jpbr->jar", stiffness[0], picked, preferred_element_type=jnp.float32)
    correction = jnp.einsum(
        "jab,jbr->jar",
        dirichlet_inv[0],
        coupled.astype(jnp.bfloat16),
        preferred_element_type=jnp.float32,
    )
    result = assembled[0] - jnp.where(shared[:, None, None], 0.0, correction)
    return result[None]


def solution(mesh):
    placed = (
        P("sub", "blk", None, None),
        P("sub", "blk", None, None, None),
        P("sub", "blk", None),
        P("sub", "blk", None, None),
        P("sub", "blk", None, None),
        P("sub", "blk", None, None),
        P("sub", None, None, None),
        P(),
    )
    return jax.shard_map(
        shards, mesh=mesh, in_specs=placed, out_specs=P("sub", "blk", None, None), check_vma=False
    )
```

profile of v0, /device:TPU:24, one launch (start us, length us, event | category | flops | bytes accessed | tf_op | source)
XLA Modules:
  0.0 186.3 jit_solution(13424925944676565091)
XLA Ops:
  6.6 2.3 %convolution_bitcast_fusion.14 = f32[192,256]{1,0:T(8,128)} fusion(bf16[1,2,375,192]{2,3,1,0:T(8,128)(2,1)} %param.13, f32[1,2,375,256]{3,1,2,0:T(2,128)} %param.8, f32[2]{0:T(128)S(1)} %get-tuple-element.5), kind=kOutput, calls=%fused_computation.31 | convolution fusion | flops 74112000 | bytes 1252616 | tf_op jit(solution)/shard_map/jbm,jbr->mr/dot_general | solution.py:42
  8.9 49.1 %all-reduce.2.cloned.1.call-done = f32[192,256]{1,0:T(8,128)} async-done(((f32[192,256]{1,0:T(8,128)}), f32[192,256]{1,0:T(8,128)}) %all-reduce.2.cloned.1.call-update) | async-done | bytes 196624 | tf_op jit(solution)/shard_map/psum | solution.py:45
  58.0 1.5 convolution_bitcast_fusion.13
  59.6 1.4 collective-permute-done
  61.7 1.6 collective-permute-start.1
  63.3 5.4 %collective-permute-done.1 = f32[192,256]{1,0:T(8,128)S(1)} collective-permute-done((f32[192,256]{1,0:T(8,128)S(1)}, f32[192,256]{1,0:T(8,128)S(1)}, u32[]{:S(2)}, u32[]{:S(2)}) %collective-permute-start.1) | collective-permute-done | bytes 196640 | tf_op jit(solution)/shard_map/ppermute | solution.py:8
  69.3 2.6 %collective-permute-start.2 = (f32[192,256]{1,0:T(8,128)S(1)}, f32[192,256]{1,0:T(8,128)S(1)}, u32[]{:S(2)}, u32[]{:S(2)}) collective-permute-start(f32[192,256]{1,0:T(8,128)S(1)} %convolution_bitcast_fusion.11), channel_id=1, source_target_pairs={{0,16},{4,20},{8,24},{12,28},{16,0},{20,4},{24,8},{28,12},{32,48},... | collective-permute-start | bytes 589832 | tf_op jit(solution)/shard_map/ppermute | solution.py:8
  71.9 8.7 %collective-permute-done.2 = f32[192,256]{1,0:T(8,128)S(1)} collective-permute-done((f32[192,256]{1,0:T(8,128)S(1)}, f32[192,256]{1,0:T(8,128)S(1)}, u32[]{:S(2)}, u32[]{:S(2)}) %collective-permute-start.2) | collective-permute-done | bytes 196640 | tf_op jit(solution)/shard_map/ppermute | solution.py:8
  81.2 5.8 %collective-permute-start.3 = (f32[192,256]{1,0:T(8,128)S(1)}, f32[192,256]{1,0:T(8,128)S(1)}, u32[]{:S(2)}, u32[]{:S(2)}) collective-permute-start(f32[192,256]{1,0:T(8,128)S(1)} %convolution_bitcast_fusion.10), channel_id=1, source_target_pairs={{0,32},{4,36},{8,40},{12,44},{16,48},{20,52},{24,56},{28,60},{32,0... | collective-permute-start | bytes 589832 | tf_op jit(solution)/shard_map/ppermute | solution.py:8
  87.0 8.0 %collective-permute-done.3 = f32[192,256]{1,0:T(8,128)S(1)} collective-permute-done((f32[192,256]{1,0:T(8,128)S(1)}, f32[192,256]{1,0:T(8,128)S(1)}, u32[]{:S(2)}, u32[]{:S(2)}) %collective-permute-start.3) | collective-permute-done | bytes 196640 | tf_op jit(solution)/shard_map/ppermute | solution.py:8
  95.6 1.5 collective-permute-start.4
  97.2 4.4 %collective-permute-done.4 = f32[192,256]{1,0:T(8,128)S(1)} collective-permute-done((f32[192,256]{1,0:T(8,128)S(1)}, f32[192,256]{1,0:T(8,128)S(1)}, u32[]{:S(2)}, u32[]{:S(2)}) %collective-permute-start.4) | collective-permute-done | bytes 196640 | tf_op jit(solution)/shard_map/ppermute | solution.py:8
  102.2 3.1 %collective-permute-start.5 = (f32[192,256]{1,0:T(8,128)S(1)}, f32[192,256]{1,0:T(8,128)S(1)}, u32[]{:S(2)}, u32[]{:S(2)}) collective-permute-start(f32[192,256]{1,0:T(8,128)S(1)} %convolution_bitcast_fusion.8), channel_id=1, source_target_pairs={{0,128},{4,132},{8,136},{12,140},{16,144},{20,148},{24,152},{28,15... | collective-permute-start | bytes 589832 | tf_op jit(solution)/shard_map/ppermute | solution.py:8
  105.3 4.2 %collective-permute-done.5 = f32[192,256]{1,0:T(8,128)S(1)} collective-permute-done((f32[192,256]{1,0:T(8,128)S(1)}, f32[192,256]{1,0:T(8,128)S(1)}, u32[]{:S(2)}, u32[]{:S(2)}) %collective-permute-start.5) | collective-permute-done | bytes 196640 | tf_op jit(solution)/shard_map/ppermute | solution.py:8
  113.2 1.3 collective-permute-start.6
  114.6 1.3 collective-permute-done.6
  116.4 1.5 collective-permute-start.7
  117.9 3.4 %collective-permute-done.7 = f32[1,375,256]{2,0,1:T(1,128)S(1)} collective-permute-done((f32[1,375,256]{2,0,1:T(1,128)S(1)}, f32[1,375,256]{2,0,1:T(1,128)S(1)}, u32[]{:S(2)}, u32[]{:S(2)}) %collective-permute-start.7) | collective-permute-done | bytes 384032 | tf_op jit(solution)/shard_map/ppermute | solution.py:14
  121.8 0.7 fusion.39
  122.5 0.8 copy.30
  123.4 38.2 %all-gather.2.cloned.1.call-done = bf16[1,8,375,256]{3,2,0,1:T(8,128)(2,1)} async-done(((bf16[1,2,375,256]{3,2,0,1:T(8,128)(2,1)}), bf16[1,8,375,256]{3,2,0,1:T(8,128)(2,1)}) %all-gather.2.cloned.1.call-update) | async-done | bytes 1536016 | tf_op jit(solution)/shard_map/all_gather | solution.py:55
  161.6 5.0 %gather_fusion = bf16[32,375,256]{2,1,0:T(8,128)(2,1)} fusion(bf16[8,375,256]{2,1,0:T(8,128)(2,1)} %bitcast.154, s32[1024]{0:T(1024)S(1)} %pad_clamp_fusion), kind=kCustom, calls=%fused_computation | custom fusion | bytes 12288128 | tf_op jit(solution)/shard_map/jit(_take)/gather | solution.py:56
  166.6 11.0 %fusion.28 = f32[2,256,375]{1,2,0:T(8,128)S(1)} fusion(bf16[2,375,375]{2,0,1:T(2,128)(2,1)S(1)} %bitcast.160, bf16[2,16,375,375]{3,1,2,0:T(8,128)(2,1)} %bitcast.159, bf16[2,16,375,256]{3,2,1,0:T(8,128)(2,1)} %bitcast.155, pred[2,16]{1,0:T(4,128)(4,1)S(1)} %compare_and_fusion), kind=kOutput, calls=%fused_computation.41 | convolution fusion | flops 2451264000 | bytes 16474532 | tf_op jit(solution)/shard_map/jab,jbr->jar/dot_general | solution.py:58
  177.7 1.8 fusion.27
  (49 shorter events, 8.0 us)
Async XLA Ops:
  6.5 105.7 %copy-start = (bf16[1,2,375,375]{3,1,2,0:T(2,128)(2,1)S(1)}, bf16[1,2,375,375]{3,1,2,0:T(2,128)(2,1)}, u32[]{:S(2)}) copy-start(bf16[1,2,375,375]{3,1,2,0:T(2,128)(2,1)} %param.11) | copy-start | bytes 1687504
  6.5 51.5 %copy-start.1 = (f32[1,6,192,192]{3,2,1,0:T(8,128)S(1)}, f32[1,6,192,192]{3,2,1,0:T(8,128)}, u32[]{:S(2)}) copy-start(f32[1,6,192,192]{3,2,1,0:T(8,128)} %param.14) | copy-start | bytes 2654212
  6.5 51.5 %all-reduce.2.cloned.1.call-start = ((), (), s32[]{:S(2)}) async-start(), calls=%async_computation | async-start | bytes 393216 | tf_op jit(solution)/shard_map/psum | solution.py:45
  8.9 152.7 %all-gather.2.cloned.1.call-start = ((), (), s32[]{:S(2)}) async-start(), calls=%async_computation.1 | async-start | bytes 1925120 | tf_op jit(solution)/shard_map/all_gather | solution.py:55
  59.5 1.5 collective-permute-start
  61.7 7.0 %collective-permute-start.1 = (f32[192,256]{1,0:T(8,128)S(1)}, f32[192,256]{1,0:T(8,128)S(1)}, u32[]{:S(2)}, u32[]{:S(2)}) collective-permute-start(f32[192,256]{1,0:T(8,128)S(1)} %convolution_bitcast_fusion.12), channel_id=1, source_target_pairs={{0,8},{4,12},{8,0},{12,4},{16,24},{20,28},{24,16},{28,20},{32,40},... | collective-permute-start | bytes 589832 | tf_op jit(solution)/shard_map/ppermute | solution.py:8
  69.3 11.3 %collective-permute-start.2 = (f32[192,256]{1,0:T(8,128)S(1)}, f32[192,256]{1,0:T(8,128)S(1)}, u32[]{:S(2)}, u32[]{:S(2)}) collective-permute-start(f32[192,256]{1,0:T(8,128)S(1)} %convolution_bitcast_fusion.11), channel_id=1, source_target_pairs={{0,16},{4,20},{8,24},{12,28},{16,0},{20,4},{24,8},{28,12},{32,48},... | collective-permute-start | bytes 589832 | tf_op jit(solution)/shard_map/ppermute | solution.py:8
  81.2 28.3 %copy-start.5 = (f32[192,192]{1,0:T(8,128)S(1)}, f32[192,192]{1,0:T(8,128)}, u32[]{:S(2)}) copy-start(f32[192,192]{1,0:T(8,128)} %param.15) | copy-start | bytes 442372
  81.2 13.8 %collective-permute-start.3 = (f32[192,256]{1,0:T(8,128)S(1)}, f32[192,256]{1,0:T(8,128)S(1)}, u32[]{:S(2)}, u32[]{:S(2)}) collective-permute-start(f32[192,256]{1,0:T(8,128)S(1)} %convolution_bitcast_fusion.10), channel_id=1, source_target_pairs={{0,32},{4,36},{8,40},{12,44},{16,48},{20,52},{24,56},{28,60},{32,0... | collective-permute-start | bytes 589832 | tf_op jit(solution)/shard_map/ppermute | solution.py:8
  95.6 6.0 %collective-permute-start.4 = (f32[192,256]{1,0:T(8,128)S(1)}, f32[192,256]{1,0:T(8,128)S(1)}, u32[]{:S(2)}, u32[]{:S(2)}) collective-permute-start(f32[192,256]{1,0:T(8,128)S(1)} %convolution_bitcast_fusion.9), channel_id=1, source_target_pairs={{0,64},{4,68},{8,72},{12,76},{16,80},{20,84},{24,88},{28,92},{32,9... | collective-permute-start | bytes 589832 | tf_op jit(solution)/shard_map/ppermute | solution.py:8
  102.2 7.3 %collective-permute-start.5 = (f32[192,256]{1,0:T(8,128)S(1)}, f32[192,256]{1,0:T(8,128)S(1)}, u32[]{:S(2)}, u32[]{:S(2)}) collective-permute-start(f32[192,256]{1,0:T(8,128)S(1)} %convolution_bitcast_fusion.8), channel_id=1, source_target_pairs={{0,128},{4,132},{8,136},{12,140},{16,144},{20,148},{24,152},{28,15... | collective-permute-start | bytes 589832 | tf_op jit(solution)/shard_map/ppermute | solution.py:8
  110.5 1.0 copy-start.4
  110.8 1.0 copy-start.3
  111.2 1.1 copy-start.2
  113.2 2.6 %collective-permute-start.6 = (f32[1,375,256]{2,0,1:T(1,128)S(1)}, f32[1,375,256]{2,0,1:T(1,128)S(1)}, u32[]{:S(2)}, u32[]{:S(2)}) collective-permute-start(f32[1,375,256]{2,0,1:T(1,128)S(1)} %bitcast.158), channel_id=1, source_target_pairs={{0,4},{4,8},{8,12},{12,16},{16,20},{20,24},{24,28},{28,32},{32,36}... | collective-permute-start | bytes 1152008 | tf_op jit(solution)/shard_map/ppermute | solution.py:14
  116.4 4.9 %collective-permute-start.7 = (f32[1,375,256]{2,0,1:T(1,128)S(1)}, f32[1,375,256]{2,0,1:T(1,128)S(1)}, u32[]{:S(2)}, u32[]{:S(2)}) collective-permute-start(f32[1,375,256]{2,0,1:T(1,128)S(1)} %fusion.36), channel_id=1, source_target_pairs={{4,0},{8,4},{12,8},{16,12},{20,16},{24,20},{28,24},{32,28},{36,32}... | collective-permute-start | bytes 1152008 | tf_op jit(solution)/shard_map/ppermute | solution.py:14
  121.8 1.5 copy-start.6
  161.6 5.0 %copy-start.7 = (bf16[1,2,375,375]{3,1,2,0:T(2,128)(2,1)S(1)}, bf16[1,2,375,375]{3,1,2,0:T(2,128)(2,1)}, u32[]{:S(2)}) copy-start(bf16[1,2,375,375]{3,1,2,0:T(2,128)(2,1)} %param.12) | copy-start | bytes 1687504
Sparse Core Ops, SparseCore 0:
  9.7 48.3 all-reduce.1
  123.4 38.1 all-gather.1
where the time goes:
time: 188 us; the launch traced here: 186 us
  waiting for transfers between devices  124 us (66%)
  matrix products  20.8 us (11%)
  starting transfers between devices  17.6 us (9%)
  between operations  13.6 us (7%)
  local copies, waits for them, and re-layouts  6.44 us (3%)
  other arithmetic  3.71 us (2%)
    psum x1, waiting for transfers between devices, shards(): total = lax.psum(partial_coarse, 'blk')  49.1 us
    all_gather x1, waiting for transfers between devices, shards(): gathered = lax.all_gather(assembled_bf, 'blk', axis=1, tiled=True)  38.2 us
    ppermute x6, waiting for transfers between devices, swapped(): lax.ppermute(x, axis, [(i, i ^ 1 << distance) for i in range(lax.axis_siz...  32.1 us
    ppermute x6, starting transfers between devices, swapped(): lax.ppermute(x, axis, [(i, i ^ 1 << distance) for i in range(lax.axis_siz...  14.8 us
    dot_general x1, matrix products, shards(): jnp.einsum('jab,jbr->jar', dirichlet_inv[0], coupled.astype(jnp.bfloat16)...  11 us
    gather x1, local copies, waits for them, and re-layouts, shards(): picked = jnp.take(gathered[0], pattern[0], axis=0)  5 us
    ppermute x2, waiting for transfers between devices, passed_along(): return lax.ppermute(x, axis, pairs)  4.69 us
    dot_general x6, matrix products, tree_solve(): own = jnp.einsum('mk,mr->kr', maps[level], current, precision=highest)  4.43 us
  transfers between devices with their start and end apart: 10, of which 10 were waited for; matrix products, arithmetic and copies ran while one was open for 0% of the time, Pallas kernels for 0%

commit v1 on v0

v1 whole, which is shorter than its diff:
```python
import jax
import jax.numpy as jnp
from jax import lax
from jax.experimental import pallas as pl
from jax.experimental.pallas import tpu as pltpu
from jax.sharding import PartitionSpec as P

MESH = pl.DeviceIdType.MESH
BF = jnp.bfloat16
F32 = jnp.float32
HIGHEST = lax.Precision.HIGHEST

GROUP = 8
ZS = 8
XS = 4


def flip(index, mask):
    out = index
    bit = 1
    while bit <= mask:
        if mask & bit:
            out = out + bit * (1 - 2 * ((index // bit) % 2))
        bit *= 2
    return out


def mm(a, b):
    return jnp.dot(a, b, precision=HIGHEST, preferred_element_type=F32)


def mmt(a, b):
    return lax.dot_general(a, b, (((1,), (1,)), ((), ())), precision=HIGHEST, preferred_element_type=F32)


def coarse_kernel(
    part, ops, root, out,
    rs_send, rs_recv, pb_send, pb_recv, w3_send, z_recv, w2_send, q3_recv, w1_send, q2_recv,
    v5_send, x_recv, v4_send, q5_recv, u_send, u_recv, q0_sum,
    rs_s, rs_r, pb_s, pb_r, z_s, z_r, q3_s, q3_r, q2_s, q2_r, x_s, x_r, q5_s, q5_r, ag_s, ag_r,
):
    s = lax.axis_index("sub")
    y = lax.axis_index("blk")
    core = s % 2
    rows = 32

    def group_peer(e):
        return {"sub": flip(s, e & 1), "blk": flip(y, e >> 1)}

    def z_peer(d):
        return {"sub": flip(s, d << 1), "blk": y}

    def x_peer(d):
        return {"sub": flip(s, d << 4), "blk": y}

    def send(src, dst, ssem, rsem, peer):
        copy = pltpu.make_async_remote_copy(
            src_ref=src, dst_ref=dst, send_sem=ssem, recv_sem=rsem, device_id=peer, device_id_type=MESH
        )
        copy.start()
        return copy

    barrier = pltpu.get_barrier_semaphore()
    peers = [group_peer(e) for e in range(1, GROUP)] + [z_peer(d) for d in range(1, ZS)] + [x_peer(d) for d in range(1, XS)]
    for peer in peers:
        pl.semaphore_signal(barrier, inc=1, device_id=peer, device_id_type=MESH)

    p = part[...]
    own0 = mm(p, ops[0])
    rs_send[...] = own0.astype(BF).reshape(GROUP, rows, own0.shape[1])
    pb_send[...] = p.astype(BF)
    pl.semaphore_wait(barrier, len(peers))

    me8 = y * 2 + core
    sent = []
    rs = []
    for e in range(1, GROUP):
        target = flip(y, e >> 1) * 2 + flip(core, e & 1)
        rs.append(send(rs_send.at[target], rs_recv.at[e], rs_s.at[e], rs_r.at[e], group_peer(e)))
    pb = []
    for e in range(1, 4):
        pb.append(send(pb_send, pb_recv.at[e], pb_s.at[e], pb_r.at[e], {"sub": s, "blk": flip(y, e)}))

    n1, n2, n3, n4, n5 = (ops[i] for i in range(1, 6))
    n12 = mm(n1, n2)
    n123 = mm(n12, n3)
    n45 = mm(n4, n5)

    for c in rs:
        c.wait_recv()
    q1 = rs_send[me8].astype(F32)
    for e in range(1, GROUP):
        q1 = q1 + rs_recv[e].astype(F32)

    w3 = mm(q1, n123)
    w3_send[...] = w3.astype(BF)
    zc = [send(w3_send, z_recv.at[d], z_s.at[d], z_r.at[d], z_peer(d)) for d in (4, 3, 5, 2, 6, 1, 7)]
    w2 = mm(q1, n12)
    w2_send[...] = w2.astype(BF)
    q3c = [send(w2_send, q3_recv.at[d], q3_s.at[d], q3_r.at[d], z_peer(d)) for d in (1, 2, 3)]
    w1 = mm(q1, n1)
    w1_send[...] = w1.astype(BF)
    q2c = [send(w1_send, q2_recv, q2_s, q2_r, z_peer(1))]

    t4 = mm(n123, n4)
    tr = mm(mm(t4, n5), root[...])

    for c in zc:
        c.wait_recv()
    q4 = w3
    for d in range(1, ZS):
        q4 = q4 + z_recv[d].astype(F32)
    v5 = mm(q4, n45)
    v5_send[...] = v5.astype(BF)
    xc = [send(v5_send, x_recv.at[d], x_s.at[d], x_r.at[d], x_peer(d)) for d in (2, 1, 3)]
    v4 = mm(q4, n4)
    v4_send[...] = v4.astype(BF)
    q5c = [send(v4_send, q5_recv, q5_s, q5_r, x_peer(1))]

    for c in q3c + q2c:
        c.wait_recv()
    q3 = w2 + q3_recv[1].astype(F32) + q3_recv[2].astype(F32) + q3_recv[3].astype(F32)
    q2 = w1 + q2_recv[...].astype(F32)
    rest = q1 + mmt(q2, n1) + mmt(q3, n12) + mmt(q4, n123)
    for c in pb:
        c.wait_recv()
    q0_sum[...] = p + pb_recv[1].astype(F32) + pb_recv[2].astype(F32) + pb_recv[3].astype(F32)

    for c in xc + q5c:
        c.wait_recv()
    q6 = v5 + x_recv[1].astype(F32) + x_recv[2].astype(F32) + x_recv[3].astype(F32)
    q5 = v4 + q5_recv[...].astype(F32)
    u1 = mmt(q6, tr) + mmt(q5, t4) + rest
    u_send[...] = u1.astype(BF)
    ag = [send(u_send, u_recv.at[me8], ag_s.at[e], ag_r.at[e], group_peer(e)) for e in (4, 5, 2, 3, 6, 7, 1)]
    u_recv[me8] = u1.astype(BF)
    for c in ag:
        c.wait_recv()
    full = u_recv[...].reshape(GROUP * rows, u1.shape[1]).astype(F32)
    u0 = mmt(full, ops[0]) + q0_sum[...]
    out[...] = u0.astype(BF)
    for c in rs + pb + zc + q3c + q2c + xc + q5c + ag:
        c.wait_send()


def coarse_solve(part, ops, root):
    loads, modes = part.shape
    chunk = (loads // GROUP, modes)
    vm = pltpu.VMEM
    dma = pltpu.SemaphoreType.DMA
    return pl.pallas_call(
        coarse_kernel,
        out_shape=jax.ShapeDtypeStruct((loads, modes), BF),
        in_specs=[pl.BlockSpec(memory_space=pltpu.VMEM)] * 3,
        out_specs=pl.BlockSpec(memory_space=pltpu.VMEM),
        scratch_shapes=[
            vm((GROUP, *chunk), BF), vm((GROUP, *chunk), BF), vm((loads, modes), BF), vm((4, loads, modes), BF),
            vm(chunk, BF), vm((ZS, *chunk), BF), vm(chunk, BF), vm((4, *chunk), BF), vm(chunk, BF), vm(chunk, BF),
            vm(chunk, BF), vm((XS, *chunk), BF), vm(chunk, BF), vm(chunk, BF), vm(chunk, BF), vm((GROUP, *chunk), BF),
            vm((loads, modes), F32),
            dma((8,)), dma((8,)), dma((4,)), dma((4,)), dma((8,)), dma((8,)), dma((4,)), dma((4,)), dma(()), dma(()),
            dma((4,)), dma((4,)), dma(()), dma(()), dma((8,)), dma((8,)),
        ],
        compiler_params=pltpu.CompilerParams(collective_id=0, has_side_effects=True),
    )(part, ops, root)


def gather_kernel(x, out, send_sem, recv_sem, local_sem):
    s = lax.axis_index("sub")
    y = lax.axis_index("blk")
    last = lax.axis_size("sub") - 1
    barrier = pltpu.get_barrier_semaphore()

    @pl.when((s == 0) | (s == last))
    def _():
        for e in range(1, 4):
            pl.semaphore_signal(barrier, inc=1, device_id={"sub": s, "blk": flip(y, e)}, device_id_type=MESH)
        own = pltpu.make_async_copy(x, out.at[y], local_sem)
        own.start()
        pl.semaphore_wait(barrier, 3)
        copies = []
        for e in (2, 1, 3):
            copy = pltpu.make_async_remote_copy(
                src_ref=x, dst_ref=out.at[y], send_sem=send_sem.at[e], recv_sem=recv_sem.at[e],
                device_id={"sub": s, "blk": flip(y, e)}, device_id_type=MESH,
            )
            copy.start()
            copies.append(copy)
        own.wait()
        for c in copies:
            c.wait_recv()
        for c in copies:
            c.wait_send()


def gather_edges(x):
    dma = pltpu.SemaphoreType.DMA
    return pl.pallas_call(
        gather_kernel,
        out_shape=jax.ShapeDtypeStruct((4, *x.shape), x.dtype),
        in_specs=[pl.BlockSpec(memory_space=pltpu.VMEM)],
        out_specs=pl.BlockSpec(memory_space=pltpu.VMEM),
        scratch_shapes=[dma((4,)), dma((4,)), dma(())],
        compiler_params=pltpu.CompilerParams(collective_id=1, has_side_effects=True),
    )(x)


def passed_along(x, axis, by):
    count = lax.axis_size(axis)
    pairs = [(i, i + by) for i in range(count) if 0 <= i + by < count]
    return lax.ppermute(x, axis, pairs)


def shards(residual, stiffness, pattern, neumann_inv, dirichlet_inv, basis, node_ops, root_inv):
    subs = lax.axis_size("sub")
    here = lax.axis_index("sub")
    per_device = residual.shape[1]
    local_ids = jnp.arange(per_device)
    shared = (local_ids == 0) & (here > 0) | (local_ids == per_device - 1) & (here < subs - 1)
    scale = jnp.where(shared, 0.5, 1.0).astype(F32)[:, None, None]
    scaled_bf = (residual[0] * scale).astype(BF)
    part = jnp.einsum("jbr,jbm->rm", scaled_bf, basis[0], preferred_element_type=F32)
    local_fix = jnp.einsum("jab,jbr->jar", neumann_inv[0], scaled_bf, preferred_element_type=F32)
    coarse_fix = coarse_solve(part, node_ops[0], root_inv)
    fix_term = jnp.einsum("jbm,rm->jbr", basis[0], coarse_fix, preferred_element_type=F32)
    combined = (local_fix + fix_term) * scale
    from_prev = passed_along(combined[-1].astype(BF), "sub", 1)
    from_next = passed_along(combined[0].astype(BF), "sub", -1)
    assembled = combined + jnp.stack([from_prev, from_next]).astype(F32)
    gathered = gather_edges(assembled.astype(BF))

    def corrected(_):
        block = jnp.where(here == 0, 0, per_device - 1)
        stiff = lax.dynamic_index_in_dim(stiffness[0], block, 0, keepdims=False)
        columns = lax.dynamic_index_in_dim(pattern[0], block, 0, keepdims=False)
        inverse = lax.dynamic_index_in_dim(dirichlet_inv[0], block, 0, keepdims=False)
        picked = jnp.take(gathered.reshape(-1, *assembled.shape[1:]), columns, axis=0)
        coupled = jnp.einsum("pab,pbr->ar", stiff, picked, preferred_element_type=F32)
        correction = jnp.dot(inverse, coupled.astype(BF), preferred_element_type=F32)
        return assembled - jnp.where(shared[:, None, None], 0.0, correction[None])

    result = lax.cond((here == 0) | (here == subs - 1), corrected, lambda _: assembled, 0)
    return result[None]


def solution(mesh):
    placed = (
        P("sub", "blk", None, None),
        P("sub", "blk", None, None, None),
        P("sub", "blk", None),
        P("sub", "blk", None, None),
        P("sub", "blk", None, None),
        P("sub", "blk", None, None),
        P("sub", None, None, None),
        P(),
    )
    return jax.shard_map(
        shards, mesh=mesh, in_specs=placed, out_specs=P("sub", "blk", None, None), check_vma=False
    )
```

time: 188 us -> 74.5 us (0.40)
  waiting for transfers between devices: 124 us -> 2.66 us
  Pallas kernels: 0 us -> 44.4 us
  starting transfers between devices: 17.6 us -> 3.47 us
  between operations: 13.6 us -> 0.16 us
  matrix products: 20.8 us -> 9.21 us
  local copies, waits for them, and re-layouts: 6.44 us -> 13 us
  other arithmetic: 3.71 us -> 1.03 us
    psum x1 -> x0, waiting for transfers between devices: 49.1 us -> none  [shards(): total = lax.psum(partial_coarse, 'blk')]
    pallas_call x0 -> x2, Pallas kernels: none -> 44.4 us  [the longest x1 30.2 us: coarse_solve(): pl.pallas_call(coarse_kernel, out_shape=jax.ShapeDtypeStruct((loads, mode...]
    all_gather x1 -> x0, waiting for transfers between devices: 38.2 us -> none  [shards(): gathered = lax.all_gather(assembled_bf, 'blk', axis=1, tiled=True)]
    ppermute x6 -> x0, waiting for transfers between devices: 32.1 us -> none  [swapped(): lax.ppermute(x, axis, [(i, i ^ 1 << distance) for i in range(lax.axis_siz...]
    ppermute x6 -> x0, starting transfers between devices: 14.8 us -> none  [swapped(): lax.ppermute(x, axis, [(i, i ^ 1 << distance) for i in range(lax.axis_siz...]
    dot_general x16 -> x3, matrix products: 20.4 us -> 8.77 us  [the longest x1 5.11 us: corrected(): jnp.dot(inverse, coupled.astype(BF), preferred_element_type=F32)]
    another operation x0 -> x2, local copies, waits for them, and re-layouts: none -> 9.32 us
    gather x1, local copies, waits for them, and re-layouts: 5 us -> 2.34 us  [corrected(): jnp.take(gathered.reshape(-1, *assembled.shape[1:]), columns, axis=0)]
  transfers between devices with their start and end apart: 10 -> 2, of which waited for: 10 -> 1; matrix products, arithmetic and copies ran while one was open for 0% -> 0% of each run, Pallas kernels for 0% -> 0%
where the time goes in v1:
time: 74.5 us; the launch traced here: 74 us
  Pallas kernels  44.4 us (60%)
  local copies, waits for them, and re-layouts  13 us (17%)
  matrix products  9.21 us (12%)
  starting transfers between devices  3.47 us (5%)
  waiting for transfers between devices  2.66 us (4%)
  other arithmetic  1.03 us (1%)
    pallas_call x1, Pallas kernels, coarse_solve(): pl.pallas_call(coarse_kernel, out_shape=jax.ShapeDtypeStruct((loads, mode...  30.2 us
    pallas_call x1, Pallas kernels, gather_edges(): pl.pallas_call(gather_kernel, out_shape=jax.ShapeDtypeStruct((4, *x.shape...  14.2 us
    another operation x2, local copies, waits for them, and re-layouts  9.32 us
    dot_general x1, matrix products, corrected(): jnp.dot(inverse, coupled.astype(BF), preferred_element_type=F32)  5.11 us
    ppermute x2, starting transfers between devices, passed_along(): return lax.ppermute(x, axis, pairs)  3.47 us
    ppermute x2, waiting for transfers between devices, passed_along(): return lax.ppermute(x, axis, pairs)  2.66 us
    dot_general x1, matrix products, shards(): jnp.einsum('jbr,jbm->rm', scaled_bf, basis[0], preferred_element_type=F32)  2.43 us
    gather x1, local copies, waits for them, and re-layouts, corrected(): jnp.take(gathered.reshape(-1, *assembled.shape[1:]), columns, axis=0)  2.34 us
  transfers between devices with their start and end apart: 2, of which 1 were waited for; matrix products, arithmetic and copies ran while one was open for 0% of the time, Pallas kernels for 0%

profile of v1, /device:TPU:24, one launch (start us, length us, event | category | flops | bytes accessed | tf_op | source)
XLA Modules:
  0.0 74.0 jit_solution(6922092447445019341)
XLA Ops:
  0.0 0.0 copy-start
  0.0 2.4 %convolution_bitcast_fusion.2.part = f32[256,192]{1,0:T(8,128)} fusion(bf16[1,2,375,192]{2,3,1,0:T(8,128)(2,1)} %param.15, f32[1,2,375,256]{3,1,2,0:T(2,128)} %param.10, f32[2]{0:T(128)S(1)} %or_select_fusion), kind=kOutput, calls=%fused_computation.26 | convolution fusion | flops 74112000 | bytes 1252616 | tf_op jit(solution)/shard_map/jbr,jbm->rm/dot_general | solution.py:222
  2.5 30.2 %shard_map.87 = bf16[256,192]{1,0:T(8,128)(2,1)} custom-call(f32[256,192]{1,0:T(8,128)} %convolution_bitcast_fusion.2.part, f32[6,192,192]{2,1,0:T(8,128)} %bitcast.65, f32[192,192]{1,0:T(8,128)} %root.1), custom_call_target="tpu_custom_call" | custom-call | tf_op jit(solution)/shard_map/pallas_call | solution.py:151
  32.7 0.0 copy-done.2
  32.7 1.2 %convolution_bitcast_fusion.1 = f32[2,375,256]{2,1,0:T(8,128)S(1)} fusion(bf16[1,2,375,192]{2,3,1,0:T(8,128)(2,1)S(1)} %copy-done.2, bf16[256,192]{1,0:T(8,128)(2,1)} %shard_map.87), kind=kOutput, calls=%fused_computation.25 | convolution fusion | flops 73728000 | bytes 1154304 | tf_op jit(solution)/shard_map/jbm,rm->jbr/dot_general | solution.py:225
  33.9 0.0 copy-done
  34.0 0.4 fusion.38
  34.4 0.0 copy-start.3
  34.4 0.0 copy-start.4
  34.5 2.2 %collective-permute-start = (bf16[375,256]{1,0:T(8,128)(2,1)S(1)}, bf16[375,256]{1,0:T(8,128)(2,1)S(1)}, u32[]{:S(2)}, u32[]{:S(2)}) collective-permute-start(bf16[375,256]{1,0:T(8,128)(2,1)S(1)} %get-tuple-element.72), channel_id=1, source_target_pairs={{0,4},{4,8},{8,12},{12,16},{16,20},{20,24},{24,28},{28,32},{32,36}... | collective-permute-start | bytes 576008 | tf_op jit(solution)/shard_map/ppermute | solution.py:211
  36.7 1.3 %collective-permute-start.1 = (bf16[375,256]{1,0:T(8,128)(2,1)S(1)}, bf16[375,256]{1,0:T(8,128)(2,1)S(1)}, u32[]{:S(2)}, u32[]{:S(2)}) collective-permute-start(bf16[375,256]{1,0:T(8,128)(2,1)S(1)} %get-tuple-element.73), channel_id=1, source_target_pairs={{4,0},{8,4},{12,8},{16,12},{20,16},{24,20},{28,24},{32,28},{36,32}... | collective-permute-start | bytes 576008 | tf_op jit(solution)/shard_map/ppermute | solution.py:211
  38.0 0.0 collective-permute-done
  38.0 2.7 %collective-permute-done.1 = bf16[375,256]{1,0:T(8,128)(2,1)S(1)} collective-permute-done((bf16[375,256]{1,0:T(8,128)(2,1)S(1)}, bf16[375,256]{1,0:T(8,128)(2,1)S(1)}, u32[]{:S(2)}, u32[]{:S(2)}) %collective-permute-start.1) | collective-permute-done | bytes 192032 | tf_op jit(solution)/shard_map/ppermute | solution.py:211
  40.6 0.8 %fusion.37 = (bf16[2,375,256]{2,1,0:T(8,128)(2,1)}, f32[2,375,256]{2,1,0:T(8,128)S(1)}) fusion(f32[2,375,256]{2,1,0:T(8,128)S(1)} %get-tuple-element.75, bf16[1,375,256]{2,1,0:T(8,128)(2,1)S(1)} %bitcast.67, bf16[1,375,256]{2,1,0:T(8,128)(2,1)S(1)} %bitcast.66), kind=kLoop, calls=%fused_computation.37 | loop fusion | flops 768000 | bytes 2304000 | tf_op jit(solution)/shard_map/convert_element_type | solution.py:230
  41.5 14.2 %shard_map.88 = bf16[4,2,375,256]{3,2,1,0:T(8,128)(2,1)S(1)} custom-call(bf16[2,375,256]{2,1,0:T(8,128)(2,1)} %get-tuple-element.70.x), custom_call_target="tpu_custom_call" | custom-call | tf_op jit(solution)/shard_map/pallas_call | solution.py:198
  55.7 0.0 copy-done.3
  55.7 0.0 copy-done.4
  55.7 18.3 %conditional.1 = (f32[1,2,375,256]{3,1,2,0:T(2,128)}) conditional(s32[]{:T(128)} %convert_element_type.23, f32[2,375,256]{2,1,0:T(8,128)S(1)} %get-tuple-element.71, (s32[2]{0:T(128)S(1)}, pred[]{:T(512)}, s32[2]{0:T(128)S(1)}, pred[]{:T(512)}, s32[]{:T(128)}, /*index=5*/bf16[1,2,375,375]{3,1,2,0:T(2,128)(2,1)S(1)}, ...), branch_computations={%region_0.1_spmd, %region_1.2_spmd} | conditional | flops 1226017152 | bytes 37104280 | solution.py:242
  55.7 2.3 %gather_fusion = bf16[16,375,256]{2,1,0:T(8,128)(2,1)} fusion(bf16[8,375,256]{2,1,0:T(8,128)(2,1)S(1)} %bitcast.63, s32[1024]{0:T(1024)S(1)} %pad_clamp_fusion), kind=kCustom, calls=%fused_computation | custom fusion | bytes 6144064 | tf_op jit(solution)/shard_map/cond/branch_1_fun/jit(_take)/gather | solution.py:237
  58.1 9.2 %copy.18 = bf16[1,2,16,375,375]{4,3,2,1,0:T(8,128)(2,1)} copy(bf16[1,2,16,375,375]{4,2,3,1,0:T(8,128)(2,1)} %get-tuple-element.65) | data formatting | bytes 18000000 | tf_op jit(solution)/shard_map
  67.3 0.1 copy.17
  67.4 5.1 %fusion.18 = f32[375,256]{1,0:T(8,128)S(1)} fusion(bf16[16,375,256]{2,1,0:T(8,128)(2,1)} %gather_fusion, pred[16]{0:T(512)(128)(4,1)S(1)} %compare_and_fusion, bf16[1,2,16,375,375]{4,3,2,1,0:T(8,128)(2,1)} %copy.18, s32[]{:T(128)S(6)} %select_n.36, bf16[1,2,375,375]{3,2,1,0:T(8,128)(2,1)S(1)} %copy.17), kind=kOutput, calls=%fused_computation.9 | convolution fusion | flops 1225632000 | bytes 8374784 | tf_op jit(solution)/shard_map/cond/branch_1_fun/dot_general | solution.py:239
  72.6 0.1 subtract_bitcast_fusion
  72.7 1.3 %copy.23 = f32[1,2,375,256]{3,1,2,0:T(2,128)} copy(f32[1,2,375,256]{3,2,1,0:T(8,128)S(1)} %subtract_bitcast_fusion) | data formatting | bytes 1536000 | tf_op jit(solution)/shard_map/cond
  (10 shorter events, 0.1 us)
Async XLA Ops:
  0.0 33.9 %copy-start = (bf16[1,2,375,375]{3,1,2,0:T(2,128)(2,1)S(1)}, bf16[1,2,375,375]{3,1,2,0:T(2,128)(2,1)}, u32[]{:S(2)}) copy-start(bf16[1,2,375,375]{3,1,2,0:T(2,128)(2,1)} %param.13) | copy-start | bytes 1687504
  0.0 34.0 %copy-start.1 = (f32[1,2,375,256]{3,1,2,0:T(2,128)S(1)}, f32[1,2,375,256]{3,1,2,0:T(2,128)}, u32[]{:S(2)}) copy-start(f32[1,2,375,256]{3,1,2,0:T(2,128)} %param.10) | copy-start | bytes 2304004
  0.0 32.7 %copy-start.2 = (bf16[1,2,375,192]{2,3,1,0:T(8,128)(2,1)S(1)}, bf16[1,2,375,192]{2,3,1,0:T(8,128)(2,1)}, u32[]{:S(2)}) copy-start(bf16[1,2,375,192]{2,3,1,0:T(8,128)(2,1)} %param.15) | copy-start | bytes 864004
  34.4 21.3 %copy-start.3 = (bf16[1,2,375,375]{3,1,2,0:T(2,128)(2,1)S(1)}, bf16[1,2,375,375]{3,1,2,0:T(2,128)(2,1)}, u32[]{:S(2)}) copy-start(bf16[1,2,375,375]{3,1,2,0:T(2,128)(2,1)} %param.14) | copy-start | bytes 1687504
  34.4 21.3 %copy-start.4 = (s32[1,2,16]{2,1,0:T(2,128)S(1)}, s32[1,2,16]{2,1,0:T(2,128)}, u32[]{:S(2)}) copy-start(s32[1,2,16]{2,1,0:T(2,128)} %param.12) | copy-start | bytes 388
  34.5 3.5 %collective-permute-start = (bf16[375,256]{1,0:T(8,128)(2,1)S(1)}, bf16[375,256]{1,0:T(8,128)(2,1)S(1)}, u32[]{:S(2)}, u32[]{:S(2)}) collective-permute-start(bf16[375,256]{1,0:T(8,128)(2,1)S(1)} %get-tuple-element.72), channel_id=1, source_target_pairs={{0,4},{4,8},{8,12},{12,16},{16,20},{20,24},{24,28},{28,32},{32,36}... | collective-permute-start | bytes 576008 | tf_op jit(solution)/shard_map/ppermute | solution.py:211
  36.7 4.0 %collective-permute-start.1 = (bf16[375,256]{1,0:T(8,128)(2,1)S(1)}, bf16[375,256]{1,0:T(8,128)(2,1)S(1)}, u32[]{:S(2)}, u32[]{:S(2)}) collective-permute-start(bf16[375,256]{1,0:T(8,128)(2,1)S(1)} %get-tuple-element.73), channel_id=1, source_target_pairs={{4,0},{8,4},{12,8},{16,12},{20,16},{24,20},{28,24},{32,28},{36,32}... | collective-permute-start | bytes 576008 | tf_op jit(solution)/shard_map/ppermute | solution.py:211

commit v2 on v1

v2 whole, which is shorter than its diff:
```python
import jax
import jax.numpy as jnp
from jax import lax
from jax.experimental import pallas as pl
from jax.experimental.pallas import tpu as pltpu
from jax.sharding import PartitionSpec as P

MESH = pl.DeviceIdType.MESH
BF = jnp.bfloat16
F32 = jnp.float32

GROUP = 8
ZS = 8
XS = 4
YS = 4
B = 375
R = 256
M = 192
CHUNK = R // GROUP


def flip(index, mask):
    out = index
    bit = 1
    while bit <= mask:
        if mask & bit:
            out = out + bit * (1 - 2 * ((index // bit) % 2))
        bit *= 2
    return out


def dot(a, b):
    return jnp.dot(a, b, preferred_element_type=F32)


def dot_t(a, b):
    return lax.dot_general(a, b, (((1,), (1,)), ((), ())), preferred_element_type=F32)


def split(a):
    high = a.astype(BF)
    return high, (a - high.astype(F32)).astype(BF)


def mm(a, b):
    (ah, al), (bh, bl) = split(a), split(b)
    return dot(ah, bh) + (dot(ah, bl) + dot(al, bh))


def mm_t(a, b):
    (ah, al), (bh, bl) = split(a), split(b)
    return dot_t(ah, bh) + (dot_t(ah, bl) + dot_t(al, bh))


def kernel(
    pattern, res, stiff, neu, diri, basis, ops_in, root_in, out,
    res_v, neu_v, bas_v, ops, root, scaled, fixed, bt, mats,
    rs_send, rs_recv, pb_send, pb_recv, w3_send, z_recv, w2_send, q3_recv, w1_send, q2_recv,
    v5_send, x_recv, v4_send, q5_recv, u_send, u_recv, uo_recv,
    m_send, mi_recv, mo_recv, t_send, ti_recv, to_recv, acc_i, acc_o,
    st_raw, st_v, dir_v, dir_b, faces,
    load, rs_s, rs_r, pb_s, pb_r, z_s, z_r, q3_s, q3_r, q2_s, q2_r, x_s, x_r, q5_s, q5_r, ag_s, ag_r, ao_s, ao_r,
    mt_s, mt_r, ed_s, ed_r,
):
    s = lax.axis_index("sub")
    y = lax.axis_index("blk")
    last = lax.axis_size("sub") - 1
    core = s % 2
    chip = s // 2
    inner = 1 - core
    outer = core
    me8 = y * 2 + core
    edge = (s == 0) | (s == last)
    has_outer = (s > 0) & (s < last)
    up, down = s - core + 2, s - core - 1
    has_up, has_down = chip < last // 2, chip > 0
    beyond = s + 2 * core - 1

    def group_peer(e):
        return {"sub": flip(s, e & 1), "blk": flip(y, e >> 1)}

    def z_peer(d):
        return {"sub": flip(s, d << 1), "blk": y}

    def x_peer(d):
        return {"sub": flip(s, d << 4), "blk": y}

    def remote(src, dst, ssem, rsem, peer):
        return pltpu.make_async_remote_copy(
            src_ref=src, dst_ref=dst, send_sem=ssem, recv_sem=rsem, device_id=peer, device_id_type=MESH
        )

    def send(*a):
        copy = remote(*a)
        copy.start()
        return copy

    loads = [
        pltpu.make_async_copy(src, dst, load.at[i])
        for i, (src, dst) in enumerate(
            [(res, res_v), (basis, bas_v), (ops_in, ops), (neu, neu_v), (root_in, root)]
        )
    ]
    for c in loads:
        c.start()
    stiff_load = pltpu.make_async_copy(stiff.at[outer], st_raw, load.at[5])
    diri_load = pltpu.make_async_copy(diri, dir_v, load.at[6])

    barrier = pltpu.get_barrier_semaphore()

    def greet(peer):
        pl.semaphore_signal(barrier, inc=1, device_id=peer, device_id_type=MESH)

    for d in (4, 3, 5, 2, 6, 1, 7):
        greet(z_peer(d))
    for d in range(1, XS):
        greet(x_peer(d))
    for e in range(1, GROUP):
        greet(group_peer(e))

    @pl.when(has_outer)
    def _():
        for e in range(YS):
            for c in range(2):
                greet({"sub": s + 3 * core - 2 + c, "blk": flip(y, e)})

    @pl.when(edge)
    def _():
        stiff_load.start()
        diri_load.start()

    outer_scale = jnp.where(edge, 1.0, 0.5).astype(F32)
    scales = [jnp.where(core == 0, outer_scale, 0.5), jnp.where(core == 0, 0.5, outer_scale)]

    loads[0].wait()
    for j in range(2):
        for h in range(2):
            scaled[j, :, h * 128 : (h + 1) * 128] = (res_v[:, h, j, :] * scales[j]).astype(BF)
    loads[1].wait()
    part = dot(bas_v[0], scaled[0]) + dot(bas_v[1], scaled[1])
    loads[2].wait()
    n0 = ops[0]
    own0 = mm(part.T, n0)
    rs_send[...] = own0.astype(BF).reshape(GROUP, CHUNK, M)
    pb_send[...] = part.astype(BF)

    senders = GROUP - 1 + ZS - 1 + XS - 1 + YS * (jnp.where(has_up, 1, 0) + jnp.where(has_down, 1, 0))
    pl.semaphore_wait(barrier, senders)

    rs = []
    for e in (4, 5, 2, 3, 6, 7, 1):
        target = flip(y, e >> 1) * 2 + flip(core, e & 1)
        rs.append(send(rs_send.at[target], rs_recv.at[e], rs_s.at[e], rs_r.at[e], group_peer(e)))
    pb = [send(pb_send, pb_recv.at[e], pb_s.at[e], pb_r.at[e], {"sub": s, "blk": flip(y, e)}) for e in (2, 1, 3)]

    n0h, n0l = split(n0)
    for j in range(2):
        bt[j] = bas_v[j].astype(F32).T.astype(BF)
        mats[j] = (dot(bt[j], n0h) + dot(bt[j], n0l)) * scales[j]
        m_send[j] = mats[j].astype(BF)
    core_peer = group_peer(1)
    mi = send(m_send.at[inner], mi_recv, mt_s.at[0], mt_r.at[0], core_peer)
    mo = remote(m_send.at[outer], mo_recv, mt_s.at[1], mt_r.at[1], {"sub": beyond, "blk": y})
    to = remote(t_send.at[outer], to_recv, mt_s.at[3], mt_r.at[3], {"sub": beyond, "blk": y})

    @pl.when(has_outer)
    def _():
        mo.start()

    loads[3].wait()
    for j in range(2):
        fixed[j] = dot(neu_v[:, j, :], scaled[j])

    n1, n2, n3, n4, n5 = (ops[i] for i in range(1, 6))
    n12 = mm(n1, n2)
    n123 = mm(n12, n3)

    for c in rs:
        c.wait_recv()
    q1 = rs_send[me8].astype(F32)
    for e in range(1, GROUP):
        q1 = q1 + rs_recv[e].astype(F32)

    w3 = mm(q1, n123)
    w3_send[...] = w3.astype(BF)
    zc = [send(w3_send, z_recv.at[d], z_s.at[d], z_r.at[d], z_peer(d)) for d in (4, 3, 5, 2, 6, 1, 7)]
    w2 = mm(q1, n12)
    w2_send[...] = w2.astype(BF)
    q3c = [send(w2_send, q3_recv.at[d], q3_s.at[d], q3_r.at[d], z_peer(d)) for d in (1, 2, 3)]
    w1 = mm(q1, n1)
    w1_send[...] = w1.astype(BF)
    q2c = [send(w1_send, q2_recv, q2_s, q2_r, z_peer(1))]

    loads[4].wait()
    n45 = mm(n4, n5)
    t4 = mm(n123, n4)
    tr = mm(mm(t4, n5), root[...])
    for c in pb:
        c.wait_recv()
    q0 = part + (pb_recv[1].astype(F32) + pb_recv[2].astype(F32) + pb_recv[3].astype(F32))
    q0h, q0l = split(q0)
    for j in range(2):
        t = (fixed[j] + (dot(bt[j], q0h) + dot(bt[j], q0l))) * scales[j]
        fixed[j] = t
        t_send[j] = t.astype(BF)
    ti = send(t_send.at[inner], ti_recv, mt_s.at[2], mt_r.at[2], core_peer)

    for c in zc:
        c.wait_recv()
    q4 = w3
    for d in range(1, ZS):
        q4 = q4 + z_recv[d].astype(F32)
    v5 = mm(q4, n45)
    v5_send[...] = v5.astype(BF)
    xc = [send(v5_send, x_recv.at[d], x_s.at[d], x_r.at[d], x_peer(d)) for d in (2, 1, 3)]
    v4 = mm(q4, n4)
    v4_send[...] = v4.astype(BF)
    q5c = [send(v4_send, q5_recv, q5_s, q5_r, x_peer(1))]

    @pl.when(has_outer)
    def _():
        to.start()

    for c in q3c + q2c:
        c.wait_recv()
    q3 = w2 + (q3_recv[1].astype(F32) + q3_recv[2].astype(F32) + q3_recv[3].astype(F32))
    q2 = w1 + q2_recv[...].astype(F32)
    rest = q1 + (mm_t(q2, n1) + (mm_t(q3, n12) + mm_t(q4, n123)))

    mi.wait_recv()
    m_inner = (mats[inner] + mi_recv[...].astype(F32)).astype(BF)
    m_outer = m_send[outer]
    ti.wait_recv()
    acc_i[...] = fixed[inner] + ti_recv[...].astype(F32)
    acc_o[...] = fixed[outer]

    @pl.when(edge)
    def _():
        stiff_load.wait()
        for i in range(0, B, 16):
            n = min(16, B - i)
            st_v[:, i : i + n, :] = jnp.swapaxes(st_raw[i : i + n], 0, 1)
        diri_load.wait()

    @pl.when(s == 0)
    def _():
        dir_b[...] = dir_v[:, 0, :]

    @pl.when(s == last)
    def _():
        dir_b[...] = dir_v[:, 1, :]

    for c in xc + q5c:
        c.wait_recv()
    q6 = v5 + (x_recv[1].astype(F32) + x_recv[2].astype(F32) + x_recv[3].astype(F32))
    q5 = v4 + q5_recv[...].astype(F32)
    u1 = mm_t(q6, tr) + mm_t(q5, t4) + rest
    u_send[...] = u1.astype(BF)
    ag = [send(u_send, u_recv.at[me8], ag_s.at[e], ag_r.at[e], group_peer(e)) for e in (4, 5, 2, 3, 6, 7, 1)]
    above = [remote(u_send, uo_recv.at[me8], ao_s.at[e], ao_r.at[me8], {"sub": up, "blk": flip(y, e)}) for e in range(YS)]
    below = [remote(u_send, uo_recv.at[me8], ao_s.at[4 + e], ao_r.at[me8], {"sub": down, "blk": flip(y, e)}) for e in range(YS)]

    @pl.when(has_up)
    def _():
        for c in above:
            c.start()

    @pl.when(has_down)
    def _():
        for c in below:
            c.start()

    u_recv[me8] = u_send[...]

    @pl.when(has_outer)
    def _():
        to.wait_recv()
        acc_o[...] += to_recv[...].astype(F32)
        mo.wait_recv()

    for c in ag:
        c.wait_recv()
    u = u_recv[...].reshape(R, M)
    acc_i[...] += dot_t(m_inner, u)
    acc_o[...] += dot_t(m_outer, u)

    @pl.when(has_outer)
    def _():
        for i in range(GROUP):
            remote(u_send, uo_recv.at[i], ao_s.at[0], ao_r.at[i], {"sub": beyond, "blk": y}).wait_recv()
        acc_o[...] += dot_t(mo_recv[...], uo_recv[...].reshape(R, M))

    @pl.when(edge)
    def _():
        faces[y * 2 + inner] = acc_i[...].astype(BF)
        faces[y * 2 + outer] = acc_o[...].astype(BF)
        copies = []
        for e in (2, 1, 3):
            for j in range(2):
                copies.append(
                    send(faces.at[y * 2 + j], faces.at[y * 2 + j], ed_s.at[e, j], ed_r.at[e, j], {"sub": s, "blk": flip(y, e)})
                )
        for c in copies:
            c.wait_recv()
        coupled = dot(st_v[0], faces[pattern[outer, 0]])
        for p in range(1, 16):
            coupled = coupled + dot(st_v[p], faces[pattern[outer, p]])
        acc_o[...] -= dot(dir_b[...], coupled.astype(BF))
        for c in copies:
            c.wait_send()

    for h in range(2):
        a, b = acc_o[:, h * 128 : (h + 1) * 128], acc_i[:, h * 128 : (h + 1) * 128]
        out[:, h, 0, :] = jnp.where(core == 0, a, b)
        out[:, h, 1, :] = jnp.where(core == 0, b, a)

    for c in rs + pb + zc + q3c + q2c + xc + q5c + ag + [mi, ti]:
        c.wait_send()

    @pl.when(has_outer)
    def _():
        mo.wait_send()
        to.wait_send()

    @pl.when(has_up)
    def _():
        for c in above:
            c.wait_send()

    @pl.when(has_down)
    def _():
        for c in below:
            c.wait_send()


def shards(residual, stiffness, pattern, neumann_inv, dirichlet_inv, basis, node_ops, root_inv):
    vm = pltpu.VMEM
    dma = pltpu.SemaphoreType.DMA
    chunk = (CHUNK, M)
    hbm = pl.BlockSpec(memory_space=pl.ANY)
    out = pl.pallas_call(
        kernel,
        out_shape=jax.ShapeDtypeStruct((B, 2, 2, 128), F32),
        in_specs=[pl.BlockSpec(memory_space=pltpu.SMEM)] + [hbm] * 7,
        out_specs=pl.BlockSpec(memory_space=pltpu.VMEM),
        scratch_shapes=[
            vm((B, 2, 2, 128), F32), vm((B, 2, B), BF), vm((2, M, B), BF), vm((6, M, M), F32), vm((M, M), F32),
            vm((2, B, R), BF), vm((2, B, R), F32), vm((2, B, M), BF), vm((2, B, M), F32),
            vm((GROUP, *chunk), BF), vm((GROUP, *chunk), BF), vm((M, R), BF), vm((4, M, R), BF),
            vm(chunk, BF), vm((ZS, *chunk), BF), vm(chunk, BF), vm((4, *chunk), BF), vm(chunk, BF), vm(chunk, BF),
            vm(chunk, BF), vm((XS, *chunk), BF), vm(chunk, BF), vm(chunk, BF), vm(chunk, BF), vm((GROUP, *chunk), BF),
            vm((GROUP, *chunk), BF),
            vm((2, B, M), BF), vm((B, M), BF), vm((B, M), BF), vm((2, B, R), BF), vm((B, R), BF), vm((B, R), BF),
            vm((B, R), F32), vm((B, R), F32),
            vm((B, 16, B), BF), vm((16, B, B), BF), vm((B, 2, B), BF), vm((B, B), BF), vm((8, B, R), BF),
            dma((7,)), dma((8,)), dma((8,)), dma((4,)), dma((4,)), dma((8,)), dma((8,)), dma((4,)), dma((4,)),
            dma(()), dma(()), dma((4,)), dma((4,)), dma(()), dma(()), dma((8,)), dma((8,)), dma((8,)), dma((8,)),
            dma((4,)), dma((4,)), dma((4, 2)), dma((4, 2)),
        ],
        compiler_params=pltpu.CompilerParams(collective_id=0, has_side_effects=True, vmem_limit_bytes=48 << 20),
    )(
        pattern[0],
        residual[0].reshape(2, B, 2, 128).transpose(1, 2, 0, 3),
        stiffness[0].transpose(0, 2, 1, 3),
        neumann_inv[0].transpose(1, 0, 2),
        dirichlet_inv[0].transpose(1, 0, 2),
        basis[0].transpose(0, 2, 1),
        node_ops[0],
        root_inv,
    )
    return out.transpose(2, 0, 1, 3).reshape(1, 2, B, R)


def solution(mesh):
    placed = (
        P("sub", "blk", None, None),
        P("sub", "blk", None, None, None),
        P("sub", "blk", None),
        P("sub", "blk", None, None),
        P("sub", "blk", None, None),
        P("sub", "blk", None, None),
        P("sub", None, None, None),
        P(),
    )
    return jax.shard_map(
        shards, mesh=mesh, in_specs=placed, out_specs=P("sub", "blk", None, None), check_vma=False
    )
```

time: 74.5 us -> 53.4 us (0.72)
  matrix products: 9.21 us -> 0 us
  local copies, waits for them, and re-layouts: 13 us -> 7.96 us
  starting transfers between devices: 3.47 us -> 0 us
  waiting for transfers between devices: 2.66 us -> 0 us
  other arithmetic: 1.03 us -> 0 us
    another operation x2 -> x0, local copies, waits for them, and re-layouts: 9.32 us -> none
    dot_general x4 -> x0, matrix products: 9.21 us -> none  [the longest x1 5.11 us: corrected(): jnp.dot(inverse, coupled.astype(BF), preferred_element_type=F32)]
    unnamed x10 -> x15, local copies, waits for them, and re-layouts: 0.02 us -> 7.96 us
    ppermute x2 -> x0, starting transfers between devices: 3.47 us -> none  [passed_along(): return lax.ppermute(x, axis, pairs)]
    ppermute x2 -> x0, waiting for transfers between devices: 2.66 us -> none  [passed_along(): return lax.ppermute(x, axis, pairs)]
    gather x1 -> x0, local copies, waits for them, and re-layouts: 2.34 us -> none  [corrected(): jnp.take(gathered.reshape(-1, *assembled.shape[1:]), columns, axis=0)]
    cond x1 -> x0, local copies, waits for them, and re-layouts: 1.27 us -> none
    convert_element_type x1 -> x0, other arithmetic: 0.84 us -> none  [shards(): gathered = gather_edges(assembled.astype(BF))]
  transfers between devices with their start and end apart: 2 -> 0, of which waited for: 1 -> 0; matrix products, arithmetic and copies ran while one was open for 0% -> 0% of each run, Pallas kernels for 0% -> 0%
where the time goes in v2:
time: 53.4 us; the launch traced here: 52.3 us
  Pallas kernels  44.4 us (83%)
  local copies, waits for them, and re-layouts  7.96 us (15%)
    pallas_call x1, Pallas kernels, shards(): pl.pallas_call(kernel, out_shape=jax.ShapeDtypeStruct((B, 2, 2, 128), F32...  44.4 us
    unnamed x15, local copies, waits for them, and re-layouts  7.96 us

profile of v2, /device:TPU:24, one launch (start us, length us, event | category | flops | bytes accessed | tf_op | source)
XLA Modules:
  0.0 52.3 jit_solution(16997966492322409015)
XLA Ops:
  0.0 0.0 copy-start
  0.0 1.3 %copy-done = f32[1,6,192,192]{3,2,1,0:T(8,128)S(1)} copy-done((f32[1,6,192,192]{3,2,1,0:T(8,128)S(1)}, f32[1,6,192,192]{3,2,1,0:T(8,128)}, u32[]{:S(2)}) %copy-start) | copy-done | bytes 884760
  1.3 0.0 copy-start.1
  1.3 1.1 %copy-done.1 = f32[1,2,375,256]{3,1,2,0:T(2,128)S(1)} copy-done((f32[1,2,375,256]{3,1,2,0:T(2,128)S(1)}, f32[1,2,375,256]{3,1,2,0:T(2,128)}, u32[]{:S(2)}) %copy-start.1) | copy-done | bytes 768024
  2.4 0.0 copy-start.2
  2.4 1.1 %copy-done.2 = bf16[1,2,375,375]{3,1,2,0:T(2,128)(2,1)S(1)} copy-done((bf16[1,2,375,375]{3,1,2,0:T(2,128)(2,1)S(1)}, bf16[1,2,375,375]{3,1,2,0:T(2,128)(2,1)}, u32[]{:S(2)}) %copy-start.2) | copy-done | bytes 562524
  3.5 0.0 copy-start.3
  3.5 1.1 %copy-done.3 = bf16[1,2,375,375]{3,1,2,0:T(2,128)(2,1)S(1)} copy-done((bf16[1,2,375,375]{3,1,2,0:T(2,128)(2,1)S(1)}, bf16[1,2,375,375]{3,1,2,0:T(2,128)(2,1)}, u32[]{:S(2)}) %copy-start.3) | copy-done | bytes 562524
  4.5 0.0 copy-start.4
  4.5 1.0 %copy-done.4 = bf16[1,2,375,192]{2,3,1,0:T(8,128)(2,1)S(1)} copy-done((bf16[1,2,375,192]{2,3,1,0:T(8,128)(2,1)S(1)}, bf16[1,2,375,192]{2,3,1,0:T(8,128)(2,1)}, u32[]{:S(2)}) %copy-start.4) | copy-done | bytes 288024
  5.5 0.0 copy-start.5
  5.5 0.9 %copy-done.5 = f32[192,192]{1,0:T(8,128)S(1)} copy-done((f32[192,192]{1,0:T(8,128)S(1)}, f32[192,192]{1,0:T(8,128)}, u32[]{:S(2)}) %copy-start.5) | copy-done | bytes 147480
  6.4 0.0 copy-start.6
  6.4 0.7 %copy-done.6 = s32[1,2,16]{2,1,0:T(2,128)S(1)} copy-done((s32[1,2,16]{2,1,0:T(2,128)S(1)}, s32[1,2,16]{2,1,0:T(2,128)}, u32[]{:S(2)}) %copy-start.6) | copy-done | bytes 152
  7.1 44.4 %shard_map.82 = f32[375,2,2,128]{3,2,1,0:T(2,128)S(1)} custom-call(s32[2,16]{1,0:T(2,128)S(1)} %bitcast.26, f32[375,2,2,128]{3,2,1,0:T(2,128)S(1)} %bitcast.22, bf16[2,375,16,375]{3,2,1,0:T(8,128)(2,1)} %bitcast.27, bf16[375,2,375]{2,1,0:T(2,128)(2,1)S(1)} %bitcast.23, bf16[375,2,375]{2,1,0:T(2,128)(2,1)S(1)} %bitcast.24, bf16[2,192,375]{2,1,0:T(8,128)(2,1)S(1)} %bitcast.25, ...), custom_call_target="tpu_custom_call" | custom-call | tf_op jit(solution)/shard_map/pallas_call | solution.py:341
  51.5 0.9 %copy.10 = f32[1,2,375,256]{3,1,2,0:T(2,128)} copy(f32[1,2,375,256]{3,1,2,0:T(2,128)S(1)} %bitcast.20) | data formatting | bytes 1536000
Async XLA Ops:
  0.0 1.3 %copy-start = (f32[1,6,192,192]{3,2,1,0:T(8,128)S(1)}, f32[1,6,192,192]{3,2,1,0:T(8,128)}, u32[]{:S(2)}) copy-start(f32[1,6,192,192]{3,2,1,0:T(8,128)} %param.14) | copy-start | bytes 2654212
  1.3 1.1 %copy-start.1 = (f32[1,2,375,256]{3,1,2,0:T(2,128)S(1)}, f32[1,2,375,256]{3,1,2,0:T(2,128)}, u32[]{:S(2)}) copy-start(f32[1,2,375,256]{3,1,2,0:T(2,128)} %param.8) | copy-start | bytes 2304004
  2.4 1.1 %copy-start.2 = (bf16[1,2,375,375]{3,1,2,0:T(2,128)(2,1)S(1)}, bf16[1,2,375,375]{3,1,2,0:T(2,128)(2,1)}, u32[]{:S(2)}) copy-start(bf16[1,2,375,375]{3,1,2,0:T(2,128)(2,1)} %param.11) | copy-start | bytes 1687504
  3.5 1.1 %copy-start.3 = (bf16[1,2,375,375]{3,1,2,0:T(2,128)(2,1)S(1)}, bf16[1,2,375,375]{3,1,2,0:T(2,128)(2,1)}, u32[]{:S(2)}) copy-start(bf16[1,2,375,375]{3,1,2,0:T(2,128)(2,1)} %param.12) | copy-start | bytes 1687504
  4.5 1.0 %copy-start.4 = (bf16[1,2,375,192]{2,3,1,0:T(8,128)(2,1)S(1)}, bf16[1,2,375,192]{2,3,1,0:T(8,128)(2,1)}, u32[]{:S(2)}) copy-start(bf16[1,2,375,192]{2,3,1,0:T(8,128)(2,1)} %param.13) | copy-start | bytes 864004
  5.5 0.9 %copy-start.5 = (f32[192,192]{1,0:T(8,128)S(1)}, f32[192,192]{1,0:T(8,128)}, u32[]{:S(2)}) copy-start(f32[192,192]{1,0:T(8,128)} %root_in.1) | copy-start | bytes 442372
  6.4 0.7 %copy-start.6 = (s32[1,2,16]{2,1,0:T(2,128)S(1)}, s32[1,2,16]{2,1,0:T(2,128)}, u32[]{:S(2)}) copy-start(s32[1,2,16]{2,1,0:T(2,128)} %param.10) | copy-start | bytes 388

commit v3 on v2

--- a/solution.py
+++ b/solution.py
@@ -58,9 +58,9 @@
     rs_send, rs_recv, pb_send, pb_recv, w3_send, z_recv, w2_send, q3_recv, w1_send, q2_recv,
     v5_send, x_recv, v4_send, q5_recv, u_send, u_recv, uo_recv,
     m_send, mi_recv, mo_recv, t_send, ti_recv, to_recv, acc_i, acc_o,
-    st_raw, st_v, dir_v, dir_b, faces,
+    st_raw, st_v, dir_v, dir_b, faces, em, et, columns,
     load, rs_s, rs_r, pb_s, pb_r, z_s, z_r, q3_s, q3_r, q2_s, q2_r, x_s, x_r, q5_s, q5_r, ag_s, ag_r, ao_s, ao_r,
-    mt_s, mt_r, ed_s, ed_r,
+    mt_s, mt_r, em_s, em_r, et_s, et_r,
 ):
     s = lax.axis_index("sub")
     y = lax.axis_index("blk")
@@ -105,6 +105,24 @@
         c.start()
     stiff_load = pltpu.make_async_copy(stiff.at[outer], st_raw, load.at[5])
     diri_load = pltpu.make_async_copy(diri, dir_v, load.at[6])
+    pattern_load = pltpu.make_async_copy(pattern, columns, load.at[7])
+
+    after = {"sub": s, "blk": (y + 1) % YS}
+    before = {"sub": s, "blk": (y + YS - 1) % YS}
+    from_before = ((y + YS - 1) % YS) * 2 + outer
+    from_after = ((y + 1) % YS) * 2 + inner
+    my_outer, my_inner = y * 2 + outer, y * 2 + inner
+
+    def ring(terms, ssem, rsem):
+        def hop(slot, i, peer):
+            return remote(terms.at[slot], terms.at[slot], ssem.at[i], rsem.at[slot], peer)
+
+        return [
+            hop(my_outer, 0, after), hop(my_outer, 1, before), hop(my_inner, 2, after), hop(my_inner, 3, before),
+            hop(from_before, 4, after), hop(from_after, 5, before),
+        ]
+
+    m_ring, t_ring = ring(em, em_s, em_r), ring(et, et_s, et_r)
 
     barrier = pltpu.get_barrier_semaphore()
 
@@ -126,6 +144,7 @@
 
     @pl.when(edge)
     def _():
+        pattern_load.start()
         stiff_load.start()
         diri_load.start()
 
@@ -167,6 +186,12 @@
     def _():
         mo.start()
 
+    @pl.when(edge)
+    def _():
+        em[my_outer] = m_send[outer]
+        m_ring[0].start()
+        m_ring[1].start()
+
     loads[3].wait()
     for j in range(2):
         fixed[j] = dot(neu_v[:, j, :], scaled[j])
@@ -191,6 +216,16 @@
     w1_send[...] = w1.astype(BF)
     q2c = [send(w1_send, q2_recv, q2_s, q2_r, z_peer(1))]
 
+    mi.wait_recv()
+    m_inner = (mats[inner] + mi_recv[...].astype(F32)).astype(BF)
+    m_outer = m_send[outer]
+
+    @pl.when(edge)
+    def _():
+        em[my_inner] = m_inner
+        m_ring[2].start()
+        m_ring[3].start()
+
     loads[4].wait()
     n45 = mm(n4, n5)
     t4 = mm(n123, n4)
@@ -204,6 +239,17 @@
         fixed[j] = t
         t_send[j] = t.astype(BF)
     ti = send(t_send.at[inner], ti_recv, mt_s.at[2], mt_r.at[2], core_peer)
+
+    def arrived(terms, ssem, rsem, slot):
+        remote(terms.at[slot], terms.at[slot], ssem.at[0], rsem.at[slot], after).wait_recv()
+
+    @pl.when(edge)
+    def _():
+        et[my_outer] = t_send[outer]
+        t_ring[0].start()
+        t_ring[1].start()
+        arrived(em, em_s, em_r, from_before)
+        m_ring[4].start()
 
     for c in zc:
         c.wait_recv()
@@ -227,28 +273,17 @@
     q2 = w1 + q2_recv[...].astype(F32)
     rest = q1 + (mm_t(q2, n1) + (mm_t(q3, n12) + mm_t(q4, n123)))
 
-    mi.wait_recv()
-    m_inner = (mats[inner] + mi_recv[...].astype(F32)).astype(BF)
-    m_outer = m_send[outer]
     ti.wait_recv()
     acc_i[...] = fixed[inner] + ti_recv[...].astype(F32)
     acc_o[...] = fixed[outer]
 
     @pl.when(edge)
     def _():
-        stiff_load.wait()
-        for i in range(0, B, 16):
-            n = min(16, B - i)
-            st_v[:, i : i + n, :] = jnp.swapaxes(st_raw[i : i + n], 0, 1)
-        diri_load.wait()
-
-    @pl.when(s == 0)
-    def _():
-        dir_b[...] = dir_v[:, 0, :]
-
-    @pl.when(s == last)
-    def _():
-        dir_b[...] = dir_v[:, 1, :]
+        et[my_inner] = acc_i[...].astype(BF)
+        t_ring[2].start()
+        t_ring[3].start()
+        arrived(em, em_s, em_r, from_after)
+        m_ring[5].start()
 
     for c in xc + q5c:
         c.wait_recv()
@@ -272,6 +307,30 @@
 
     u_recv[me8] = u_send[...]
 
+    @pl.when(edge)
+    def _():
+        arrived(et, et_s, et_r, from_before)
+        t_ring[4].start()
+        arrived(et, et_s, et_r, from_after)
+        t_ring[5].start()
+
+    @pl.when(edge)
+    def _():
+        stiff_load.wait()
+        for i in range(0, B, 16):
+            n = min(16, B - i)
+            st_v[:, i : i + n, :] = jnp.swapaxes(st_raw[i : i + n], 0, 1)
+        diri_load.wait()
+        pattern_load.wait()
+
+    @pl.when(s == 0)
+    def _():
+        dir_b[...] = dir_v[:, 0, :]
+
+    @pl.when(s == last)
+    def _():
+        dir_b[...] = dir_v[:, 1, :]
+
     @pl.when(has_outer)
     def _():
         to.wait_recv()
@@ -292,21 +351,22 @@
 
     @pl.when(edge)
     def _():
-        faces[y * 2 + inner] = acc_i[...].astype(BF)
-        faces[y * 2 + outer] = acc_o[...].astype(BF)
-        copies = []
-        for e in (2, 1, 3):
+        for e in range(1, YS):
             for j in range(2):
-                copies.append(
-                    send(faces.at[y * 2 + j], faces.at[y * 2 + j], ed_s.at[e, j], ed_r.at[e, j], {"sub": s, "blk": flip(y, e)})
-                )
-        for c in copies:
-            c.wait_recv()
-        coupled = dot(st_v[0], faces[pattern[outer, 0]])
+                slot = ((y + e) % YS) * 2 + j
+
+                @pl.when((slot != from_before) & (slot != from_after))
+                def _():
+                    arrived(em, em_s, em_r, slot)
+                    arrived(et, et_s, et_r, slot)
+
+        for j in range(8):
+            faces[j] = (et[j].astype(F32) + dot_t(em[j], u)).astype(BF)
+        coupled = dot(st_v[0], faces[columns[outer, 0]])
         for p in range(1, 16):
-            coupled = coupled + dot(st_v[p], faces[pattern[outer, p]])
+            coupled = coupled + dot(st_v[p], faces[columns[outer, p]])
         acc_o[...] -= dot(dir_b[...], coupled.astype(BF))
-        for c in copies:
+        for c in m_ring + t_ring:
             c.wait_send()
 
     for h in range(2):
@@ -341,7 +401,7 @@
     out = pl.pallas_call(
         kernel,
         out_shape=jax.ShapeDtypeStruct((B, 2, 2, 128), F32),
-        in_specs=[pl.BlockSpec(memory_space=pltpu.SMEM)] + [hbm] * 7,
+        in_specs=[hbm] * 8,
         out_specs=pl.BlockSpec(memory_space=pltpu.VMEM),
         scratch_shapes=[
             vm((B, 2, 2, 128), F32), vm((B, 2, B), BF), vm((2, M, B), BF), vm((6, M, M), F32), vm((M, M), F32),
@@ -353,20 +413,21 @@
             vm((2, B, M), BF), vm((B, M), BF), vm((B, M), BF), vm((2, B, R), BF), vm((B, R), BF), vm((B, R), BF),
             vm((B, R), F32), vm((B, R), F32),
             vm((B, 16, B), BF), vm((16, B, B), BF), vm((B, 2, B), BF), vm((B, B), BF), vm((8, B, R), BF),
-            dma((7,)), dma((8,)), dma((8,)), dma((4,)), dma((4,)), dma((8,)), dma((8,)), dma((4,)), dma((4,)),
+            vm((8, B, M), BF), vm((8, B, R), BF), pltpu.SMEM((2, 16), jnp.int32),
+            dma((8,)), dma((8,)), dma((8,)), dma((4,)), dma((4,)), dma((8,)), dma((8,)), dma((4,)), dma((4,)),
             dma(()), dma(()), dma((4,)), dma((4,)), dma(()), dma(()), dma((8,)), dma((8,)), dma((8,)), dma((8,)),
-            dma((4,)), dma((4,)), dma((4, 2)), dma((4, 2)),
+            dma((4,)), dma((4,)), dma((6,)), dma((8,)), dma((6,)), dma((8,)),
         ],
         compiler_params=pltpu.CompilerParams(collective_id=0, has_side_effects=True, vmem_limit_bytes=48 << 20),
     )(
-        pattern[0],
-        residual[0].reshape(2, B, 2, 128).transpose(1, 2, 0, 3),
-        stiffness[0].transpose(0, 2, 1, 3),
-        neumann_inv[0].transpose(1, 0, 2),
-        dirichlet_inv[0].transpose(1, 0, 2),
-        basis[0].transpose(0, 2, 1),
-        node_ops[0],
-        root_inv,
+        pltpu.with_memory_space_constraint(pattern[0], pltpu.HBM),
+        pltpu.with_memory_space_constraint(residual[0].reshape(2, B, 2, 128).transpose(1, 2, 0, 3), pltpu.HBM),
+        pltpu.with_memory_space_constraint(stiffness[0].transpose(0, 2, 1, 3), pltpu.HBM),
+        pltpu.with_memory_space_constraint(neumann_inv[0].transpose(1, 0, 2), pltpu.HBM),
+        pltpu.with_memory_space_constraint(dirichlet_inv[0].transpose(1, 0, 2), pltpu.HBM),
+        pltpu.with_memory_space_constraint(basis[0].transpose(0, 2, 1), pltpu.HBM),
+        pltpu.with_memory_space_constraint(node_ops[0], pltpu.HBM),
+        pltpu.with_memory_space_constraint(root_inv, pltpu.HBM),
     )
     return out.transpose(2, 0, 1, 3).reshape(1, 2, B, R)
 

time: 53.4 us -> 37.3 us (0.70); the launches traced: 52.3 us -> 37.3 us
  Pallas kernels: 44.4 us -> 36.4 us
  local copies, waits for them, and re-layouts: 7.96 us -> 0.88 us
    pallas_call x1, Pallas kernels: 44.4 us -> 36.4 us  [shards(): pl.pallas_call(kernel, out_shape=jax.ShapeDtypeStruct((B, 2, 2, 128), F32...]
    unnamed x15 -> x1, local copies, waits for them, and re-layouts: 7.96 us -> 0.88 us
where the time goes in v3:
time: 37.3 us
  Pallas kernels  36.4 us (98%)
  local copies, waits for them, and re-layouts  0.88 us (2%)
    pallas_call x1, Pallas kernels, shards(): pl.pallas_call(kernel, out_shape=jax.ShapeDtypeStruct((B, 2, 2, 128), F32...  36.4 us
    unnamed x1, local copies, waits for them, and re-layouts  0.88 us

profile of v3, /device:TPU:24, one launch (start us, length us, event | category | flops | bytes accessed | tf_op | source)
XLA Modules:
  0.0 37.3 jit_solution(11755761941190345933)
XLA Ops:
  0.0 36.4 %shard_map.82 = f32[375,2,2,128]{3,2,1,0:T(2,128)S(1)} custom-call(s32[2,16]{1,0:T(2,128)} %bitcast.27, f32[375,2,2,128]{3,2,1,0:T(2,128)} %bitcast.23, bf16[2,375,16,375]{3,2,1,0:T(8,128)(2,1)} %bitcast.21, bf16[375,2,375]{2,1,0:T(2,128)(2,1)} %bitcast.24, bf16[375,2,375]{2,1,0:T(2,128)(2,1)} %bitcast.25, bf16[2,192,375]{2,1,0:T(8,128)(2,1)} %bitcast.26, ...), custom_call_target="tpu_custom_call" | custom-call | tf_op jit(solution)/shard_map/pallas_call | solution.py:401
  36.4 0.9 %copy.10 = f32[1,2,375,256]{3,1,2,0:T(2,128)} copy(f32[1,2,375,256]{3,1,2,0:T(2,128)S(1)} %bitcast.20) | data formatting | bytes 1536000

commit v4 on v3

--- a/solution.py
+++ b/solution.py
@@ -55,11 +55,11 @@
 def kernel(
     pattern, res, stiff, neu, diri, basis, ops_in, root_in, out,
     res_v, neu_v, bas_v, ops, root, scaled, fixed, bt, mats,
-    rs_send, rs_recv, pb_send, pb_recv, w3_send, z_recv, w2_send, q3_recv, w1_send, q2_recv,
+    rs_send, rs_recv, p_own, p_send, p_recv, q0_send, q0_recv, w3_send, z_recv, w2_send, q3_recv, w1_send, q2_recv,
     v5_send, x_recv, v4_send, q5_recv, u_send, u_recv, uo_recv,
     m_send, mi_recv, mo_recv, t_send, ti_recv, to_recv, acc_i, acc_o,
-    st_raw, st_v, dir_v, dir_b, faces, em, et, columns,
-    load, rs_s, rs_r, pb_s, pb_r, z_s, z_r, q3_s, q3_r, q2_s, q2_r, x_s, x_r, q5_s, q5_r, ag_s, ag_r, ao_s, ao_r,
+    st_raw, sums, dir_v, dir_b, mixed, terms, em, et, columns, mix, mix_tail,
+    load, rs_s, rs_r, ps_s, ps_r, q0_s, q0_r, z_s, z_r, q3_s, q3_r, q2_s, q2_r, x_s, x_r, q5_s, q5_r, ag_s, ag_r, ao_s, ao_r,
     mt_s, mt_r, em_s, em_r, et_s, et_r,
 ):
     s = lax.axis_index("sub")
@@ -159,9 +159,11 @@
     part = dot(bas_v[0], scaled[0]) + dot(bas_v[1], scaled[1])
     loads[2].wait()
     n0 = ops[0]
-    own0 = mm(part.T, n0)
+    part = part.T
+    own0 = mm(part, n0)
     rs_send[...] = own0.astype(BF).reshape(GROUP, CHUNK, M)
-    pb_send[...] = part.astype(BF)
+    p_own[...] = part.reshape(YS, R // YS, M)
+    p_send[...] = part.astype(BF).reshape(YS, R // YS, M)
 
     senders = GROUP - 1 + ZS - 1 + XS - 1 + YS * (jnp.where(has_up, 1, 0) + jnp.where(has_down, 1, 0))
     pl.semaphore_wait(barrier, senders)
@@ -170,7 +172,9 @@
     for e in (4, 5, 2, 3, 6, 7, 1):
         target = flip(y, e >> 1) * 2 + flip(core, e & 1)
         rs.append(send(rs_send.at[target], rs_recv.at[e], rs_s.at[e], rs_r.at[e], group_peer(e)))
-    pb = [send(pb_send, pb_recv.at[e], pb_s.at[e], pb_r.at[e], {"sub": s, "blk": flip(y, e)}) for e in (2, 1, 3)]
+    ps = [
+        send(p_send.at[flip(y, e)], p_recv.at[e], ps_s.at[e], ps_r.at[e], {"sub": s, "blk": flip(y, e)}) for e in (2, 1, 3)
+    ]
 
     n0h, n0l = split(n0)
     for j in range(2):
@@ -200,6 +204,43 @@
     n12 = mm(n1, n2)
     n123 = mm(n12, n3)
 
+    mi.wait_recv()
+    m_inner = (mats[inner] + mi_recv[...].astype(F32)).astype(BF)
+    m_outer = m_send[outer]
+
+    @pl.when(edge)
+    def _():
+        em[my_inner] = m_inner
+        m_ring[2].start()
+        m_ring[3].start()
+
+    def arrived(terms, ssem, rsem, slot):
+        remote(terms.at[slot], terms.at[slot], ssem.at[0], rsem.at[slot], after).wait_recv()
+
+    def mixing(n, padded):
+        row = lax.broadcasted_iota(jnp.int32, (8 * padded, 16 * n), 0)
+        col = lax.broadcasted_iota(jnp.int32, (8 * padded, 16 * n), 1)
+        spread = lax.broadcasted_iota(jnp.int32, (16, 16 * n), 0) == lax.broadcasted_iota(jnp.int32, (16, 16 * n), 1) % 16
+        both = dot(columns[...].astype(F32).astype(BF), jnp.where(spread, 1.0, 0.0).astype(BF))
+        wanted = jnp.where(core == 0, both[0:1], both[1:2])
+        hit = ((row // padded).astype(F32) == wanted) & (row % padded == col // 16)
+        return jnp.where(hit, 1.0, 0.0).astype(BF)
+
+    def mix_rows(begin, end):
+        for i in range(begin, end, 16):
+            n = min(16, end - i)
+            weights, padded = (mix[...], 16) if n == 16 else (mix_tail[...], 8)
+            rows = dot(weights, st_raw[i : i + n].reshape(16 * n, B)).astype(BF).reshape(8, padded, B)
+            sums[:, i : i + n, :] = rows[:, :n]
+
+    @pl.when(edge)
+    def _():
+        pattern_load.wait()
+        stiff_load.wait()
+        mix[...] = mixing(16, 16)
+        mix_tail[...] = mixing(B % 16, 8)
+        mix_rows(0, 192)
+
     for c in rs:
         c.wait_recv()
     q1 = rs_send[me8].astype(F32)
@@ -209,6 +250,13 @@
     w3 = mm(q1, n123)
     w3_send[...] = w3.astype(BF)
     zc = [send(w3_send, z_recv.at[d], z_s.at[d], z_r.at[d], z_peer(d)) for d in (4, 3, 5, 2, 6, 1, 7)]
+    for c in ps:
+        c.wait_recv()
+    own_q0 = p_own[y] + (p_recv[1].astype(F32) + p_recv[2].astype(F32) + p_recv[3].astype(F32))
+    q0_send[...] = own_q0.astype(BF)
+    qs = [send(q0_send, q0_recv.at[y], q0_s.at[e], q0_r.at[e], {"sub": s, "blk": flip(y, e)}) for e in (2, 1, 3)]
+    q0_recv[y] = own_q0.astype(BF)
+
     w2 = mm(q1, n12)
     w2_send[...] = w2.astype(BF)
     q3c = [send(w2_send, q3_recv.at[d], q3_s.at[d], q3_r.at[d], z_peer(d)) for d in (1, 2, 3)]
@@ -216,40 +264,40 @@
     w1_send[...] = w1.astype(BF)
     q2c = [send(w1_send, q2_recv, q2_s, q2_r, z_peer(1))]
 
-    mi.wait_recv()
-    m_inner = (mats[inner] + mi_recv[...].astype(F32)).astype(BF)
-    m_outer = m_send[outer]
-
-    @pl.when(edge)
-    def _():
-        em[my_inner] = m_inner
-        m_ring[2].start()
-        m_ring[3].start()
+    @pl.when(edge)
+    def _():
+        arrived(em, em_s, em_r, from_before)
+        m_ring[4].start()
+        arrived(em, em_s, em_r, from_after)
+        m_ring[5].start()
+        mix_rows(192, B)
 
     loads[4].wait()
     n45 = mm(n4, n5)
     t4 = mm(n123, n4)
     tr = mm(mm(t4, n5), root[...])
-    for c in pb:
-        c.wait_recv()
-    q0 = part + (pb_recv[1].astype(F32) + pb_recv[2].astype(F32) + pb_recv[3].astype(F32))
-    q0h, q0l = split(q0)
+    for c in qs:
+        c.wait_recv()
+    q0 = q0_recv[...].reshape(R, M)
     for j in range(2):
-        t = (fixed[j] + (dot(bt[j], q0h) + dot(bt[j], q0l))) * scales[j]
+        t = (fixed[j] + dot_t(bt[j], q0)) * scales[j]
         fixed[j] = t
         t_send[j] = t.astype(BF)
     ti = send(t_send.at[inner], ti_recv, mt_s.at[2], mt_r.at[2], core_peer)
 
-    def arrived(terms, ssem, rsem, slot):
-        remote(terms.at[slot], terms.at[slot], ssem.at[0], rsem.at[slot], after).wait_recv()
+    def inner_terms():
+        ti.wait_recv()
+        acc_i[...] = fixed[inner] + ti_recv[...].astype(F32)
 
     @pl.when(edge)
     def _():
         et[my_outer] = t_send[outer]
         t_ring[0].start()
         t_ring[1].start()
-        arrived(em, em_s, em_r, from_before)
-        m_ring[4].start()
+        inner_terms()
+        et[my_inner] = acc_i[...].astype(BF)
+        t_ring[2].start()
+        t_ring[3].start()
 
     for c in zc:
         c.wait_recv()
@@ -273,17 +321,28 @@
     q2 = w1 + q2_recv[...].astype(F32)
     rest = q1 + (mm_t(q2, n1) + (mm_t(q3, n12) + mm_t(q4, n123)))
 
-    ti.wait_recv()
-    acc_i[...] = fixed[inner] + ti_recv[...].astype(F32)
     acc_o[...] = fixed[outer]
 
-    @pl.when(edge)
-    def _():
-        et[my_inner] = acc_i[...].astype(BF)
-        t_ring[2].start()
-        t_ring[3].start()
-        arrived(em, em_s, em_r, from_after)
-        m_ring[5].start()
+    @pl.when(s * (last - s) > 0)
+    def _():
+        inner_terms()
+
+    near = [my_outer, my_inner, from_before, from_after]
+    far = [
+        ((y + YS - 1) % YS) * 2 + inner, ((y + 1) % YS) * 2 + outer, ((y + 2) % YS) * 2 + outer, ((y + 2) % YS) * 2 + inner,
+    ]
+
+    @pl.when(edge)
+    def _():
+        diri_load.wait()
+
+    @pl.when(s == 0)
+    def _():
+        dir_b[...] = dir_v[:, 0, :]
+
+    @pl.when(s == last)
+    def _():
+        dir_b[...] = dir_v[:, 1, :]
 
     for c in xc + q5c:
         c.wait_recv()
@@ -311,25 +370,18 @@
     def _():
         arrived(et, et_s, et_r, from_before)
         t_ring[4].start()
+        for slot in far:
+            arrived(em, em_s, em_r, slot)
+        total = dot(sums[my_outer], em[my_outer])
+        for slot in near[1:] + far:
+            total = total + dot(sums[slot], em[slot])
+        mixed[...] = total.astype(BF)
         arrived(et, et_s, et_r, from_after)
         t_ring[5].start()
-
-    @pl.when(edge)
-    def _():
-        stiff_load.wait()
-        for i in range(0, B, 16):
-            n = min(16, B - i)
-            st_v[:, i : i + n, :] = jnp.swapaxes(st_raw[i : i + n], 0, 1)
-        diri_load.wait()
-        pattern_load.wait()
-
-    @pl.when(s == 0)
-    def _():
-        dir_b[...] = dir_v[:, 0, :]
-
-    @pl.when(s == last)
-    def _():
-        dir_b[...] = dir_v[:, 1, :]
+        total = dot(sums[my_outer], et[my_outer])
+        for slot in near[1:]:
+            total = total + dot(sums[slot], et[slot])
+        terms[...] = total
 
     @pl.when(has_outer)
     def _():
@@ -351,20 +403,10 @@
 
     @pl.when(edge)
     def _():
-        for e in range(1, YS):
-            for j in range(2):
-                slot = ((y + e) % YS) * 2 + j
-
-                @pl.when((slot != from_before) & (slot != from_after))
-                def _():
-                    arrived(em, em_s, em_r, slot)
-                    arrived(et, et_s, et_r, slot)
-
-        for j in range(8):
-            faces[j] = (et[j].astype(F32) + dot_t(em[j], u)).astype(BF)
-        coupled = dot(st_v[0], faces[columns[outer, 0]])
-        for p in range(1, 16):
-            coupled = coupled + dot(st_v[p], faces[columns[outer, p]])
+        for slot in far:
+            arrived(et, et_s, et_r, slot)
+            terms[...] += dot(sums[slot], et[slot])
+        coupled = terms[...] + dot_t(mixed[...], u)
         acc_o[...] -= dot(dir_b[...], coupled.astype(BF))
         for c in m_ring + t_ring:
             c.wait_send()
@@ -374,7 +416,7 @@
         out[:, h, 0, :] = jnp.where(core == 0, a, b)
         out[:, h, 1, :] = jnp.where(core == 0, b, a)
 
-    for c in rs + pb + zc + q3c + q2c + xc + q5c + ag + [mi, ti]:
+    for c in rs + ps + qs + zc + q3c + q2c + xc + q5c + ag + [mi, ti]:
         c.wait_send()
 
     @pl.when(has_outer)
@@ -406,15 +448,16 @@
         scratch_shapes=[
             vm((B, 2, 2, 128), F32), vm((B, 2, B), BF), vm((2, M, B), BF), vm((6, M, M), F32), vm((M, M), F32),
             vm((2, B, R), BF), vm((2, B, R), F32), vm((2, B, M), BF), vm((2, B, M), F32),
-            vm((GROUP, *chunk), BF), vm((GROUP, *chunk), BF), vm((M, R), BF), vm((4, M, R), BF),
+            vm((GROUP, *chunk), BF), vm((GROUP, *chunk), BF), vm((YS, R // YS, M), F32), vm((YS, R // YS, M), BF), vm((YS, R // YS, M), BF),
+            vm((R // YS, M), BF), vm((YS, R // YS, M), BF),
             vm(chunk, BF), vm((ZS, *chunk), BF), vm(chunk, BF), vm((4, *chunk), BF), vm(chunk, BF), vm(chunk, BF),
             vm(chunk, BF), vm((XS, *chunk), BF), vm(chunk, BF), vm(chunk, BF), vm(chunk, BF), vm((GROUP, *chunk), BF),
             vm((GROUP, *chunk), BF),
             vm((2, B, M), BF), vm((B, M), BF), vm((B, M), BF), vm((2, B, R), BF), vm((B, R), BF), vm((B, R), BF),
             vm((B, R), F32), vm((B, R), F32),
-            vm((B, 16, B), BF), vm((16, B, B), BF), vm((B, 2, B), BF), vm((B, B), BF), vm((8, B, R), BF),
-            vm((8, B, M), BF), vm((8, B, R), BF), pltpu.SMEM((2, 16), jnp.int32),
-            dma((8,)), dma((8,)), dma((8,)), dma((4,)), dma((4,)), dma((8,)), dma((8,)), dma((4,)), dma((4,)),
+            vm((B, 16, B), BF), vm((8, B, B), BF), vm((B, 2, B), BF), vm((B, B), BF), vm((B, M), BF), vm((B, R), F32),
+            vm((8, B, M), BF), vm((8, B, R), BF), vm((2, 16), jnp.int32), vm((128, 256), BF), vm((64, 112), BF),
+            dma((8,)), dma((8,)), dma((8,)), dma((4,)), dma((4,)), dma((4,)), dma((4,)), dma((8,)), dma((8,)), dma((4,)), dma((4,)),
             dma(()), dma(()), dma((4,)), dma((4,)), dma(()), dma(()), dma((8,)), dma((8,)), dma((8,)), dma((8,)),
             dma((4,)), dma((4,)), dma((6,)), dma((8,)), dma((6,)), dma((8,)),
         ],

time: 37.3 us -> 34.6 us (0.928)
  Pallas kernels: 36.4 us -> 33.6 us
    pallas_call x1, Pallas kernels: 36.4 us -> 33.6 us  [shards(): pl.pallas_call(kernel, out_shape=jax.ShapeDtypeStruct((B, 2, 2, 128), F32...]
where the time goes in v4:
time: 34.6 us; the launch traced here: 34.4 us
  Pallas kernels  33.6 us (97%)
  local copies, waits for them, and re-layouts  0.88 us (3%)
    pallas_call x1, Pallas kernels, shards(): pl.pallas_call(kernel, out_shape=jax.ShapeDtypeStruct((B, 2, 2, 128), F32...  33.6 us
    unnamed x1, local copies, waits for them, and re-layouts  0.88 us

profile of v4, /device:TPU:24, one launch (start us, length us, event | category | flops | bytes accessed | tf_op | source)
XLA Modules:
  0.0 34.4 jit_solution(7380843852969248884)
XLA Ops:
  0.0 33.6 %shard_map.82 = f32[375,2,2,128]{3,2,1,0:T(2,128)S(1)} custom-call(s32[2,16]{1,0:T(2,128)} %bitcast.27, f32[375,2,2,128]{3,2,1,0:T(2,128)} %bitcast.23, bf16[2,375,16,375]{3,2,1,0:T(8,128)(2,1)} %bitcast.21, bf16[375,2,375]{2,1,0:T(2,128)(2,1)} %bitcast.24, bf16[375,2,375]{2,1,0:T(2,128)(2,1)} %bitcast.25, bf16[2,192,375]{2,1,0:T(8,128)(2,1)} %bitcast.26, ...), custom_call_target="tpu_custom_call" | custom-call | tf_op jit(solution)/shard_map/pallas_call | solution.py:443
  33.6 0.9 %copy.10 = f32[1,2,375,256]{3,1,2,0:T(2,128)} copy(f32[1,2,375,256]{3,1,2,0:T(2,128)S(1)} %bitcast.20) | data formatting | bytes 1536000

commit v5 on v4

--- a/solution.py
+++ b/solution.py
@@ -40,6 +40,18 @@
 def split(a):
     high = a.astype(BF)
     return high, (a - high.astype(F32)).astype(BF)
+
+
+def pack(x):
+    low, high = x[..., :128], x[..., 128:]
+    half = x.shape[-2] // 2
+    return jnp.concatenate([low, jnp.concatenate([high[..., :half, :], high[..., half:, :]], axis=-1)], axis=-2)
+
+
+def unpack(x):
+    n = x.shape[-2] * 2 // 3
+    low, high = x[..., :n, :], x[..., n:, :]
+    return jnp.concatenate([low, jnp.concatenate([high[..., :64], high[..., 64:]], axis=-2)], axis=-1)
 
 
 def mm(a, b):
@@ -161,9 +173,10 @@
     n0 = ops[0]
     part = part.T
     own0 = mm(part, n0)
-    rs_send[...] = own0.astype(BF).reshape(GROUP, CHUNK, M)
-    p_own[...] = part.reshape(YS, R // YS, M)
-    p_send[...] = part.astype(BF).reshape(YS, R // YS, M)
+    rs_send[...] = pack(own0.reshape(GROUP, CHUNK, M)).astype(BF)
+    parts = pack(part.reshape(YS, R // YS, M))
+    p_own[...] = parts
+    p_send[...] = parts.astype(BF)
 
     senders = GROUP - 1 + ZS - 1 + XS - 1 + YS * (jnp.where(has_up, 1, 0) + jnp.where(has_down, 1, 0))
     pl.semaphore_wait(barrier, senders)
@@ -246,8 +259,10 @@
     q1 = rs_send[me8].astype(F32)
     for e in range(1, GROUP):
         q1 = q1 + rs_recv[e].astype(F32)
+    q1 = unpack(q1)
 
     w3 = mm(q1, n123)
+    w3 = pack(w3)
     w3_send[...] = w3.astype(BF)
     zc = [send(w3_send, z_recv.at[d], z_s.at[d], z_r.at[d], z_peer(d)) for d in (4, 3, 5, 2, 6, 1, 7)]
     for c in ps:
@@ -258,9 +273,11 @@
     q0_recv[y] = own_q0.astype(BF)
 
     w2 = mm(q1, n12)
+    w2 = pack(w2)
     w2_send[...] = w2.astype(BF)
     q3c = [send(w2_send, q3_recv.at[d], q3_s.at[d], q3_r.at[d], z_peer(d)) for d in (1, 2, 3)]
     w1 = mm(q1, n1)
+    w1 = pack(w1)
     w1_send[...] = w1.astype(BF)
     q2c = [send(w1_send, q2_recv, q2_s, q2_r, z_peer(1))]
 
@@ -278,7 +295,7 @@
     tr = mm(mm(t4, n5), root[...])
     for c in qs:
         c.wait_recv()
-    q0 = q0_recv[...].reshape(R, M)
+    q0 = unpack(q0_recv[...]).reshape(R, M)
     for j in range(2):
         t = (fixed[j] + dot_t(bt[j], q0)) * scales[j]
         fixed[j] = t
@@ -304,10 +321,13 @@
     q4 = w3
     for d in range(1, ZS):
         q4 = q4 + z_recv[d].astype(F32)
+    q4 = unpack(q4)
     v5 = mm(q4, n45)
+    v5 = pack(v5)
     v5_send[...] = v5.astype(BF)
     xc = [send(v5_send, x_recv.at[d], x_s.at[d], x_r.at[d], x_peer(d)) for d in (2, 1, 3)]
     v4 = mm(q4, n4)
+    v4 = pack(v4)
     v4_send[...] = v4.astype(BF)
     q5c = [send(v4_send, q5_recv, q5_s, q5_r, x_peer(1))]
 
@@ -317,8 +337,8 @@
 
     for c in q3c + q2c:
         c.wait_recv()
-    q3 = w2 + (q3_recv[1].astype(F32) + q3_recv[2].astype(F32) + q3_recv[3].astype(F32))
-    q2 = w1 + q2_recv[...].astype(F32)
+    q3 = unpack(w2 + (q3_recv[1].astype(F32) + q3_recv[2].astype(F32) + q3_recv[3].astype(F32)))
+    q2 = unpack(w1 + q2_recv[...].astype(F32))
     rest = q1 + (mm_t(q2, n1) + (mm_t(q3, n12) + mm_t(q4, n123)))
 
     acc_o[...] = fixed[outer]
@@ -346,10 +366,10 @@
 
     for c in xc + q5c:
         c.wait_recv()
-    q6 = v5 + (x_recv[1].astype(F32) + x_recv[2].astype(F32) + x_recv[3].astype(F32))
-    q5 = v4 + q5_recv[...].astype(F32)
+    q6 = unpack(v5 + (x_recv[1].astype(F32) + x_recv[2].astype(F32) + x_recv[3].astype(F32)))
+    q5 = unpack(v4 + q5_recv[...].astype(F32))
     u1 = mm_t(q6, tr) + mm_t(q5, t4) + rest
-    u_send[...] = u1.astype(BF)
+    u_send[...] = pack(u1).astype(BF)
     ag = [send(u_send, u_recv.at[me8], ag_s.at[e], ag_r.at[e], group_peer(e)) for e in (4, 5, 2, 3, 6, 7, 1)]
     above = [remote(u_send, uo_recv.at[me8], ao_s.at[e], ao_r.at[me8], {"sub": up, "blk": flip(y, e)}) for e in range(YS)]
     below = [remote(u_send, uo_recv.at[me8], ao_s.at[4 + e], ao_r.at[me8], {"sub": down, "blk": flip(y, e)}) for e in range(YS)]
@@ -391,7 +411,7 @@
 
     for c in ag:
         c.wait_recv()
-    u = u_recv[...].reshape(R, M)
+    u = unpack(u_recv[...]).reshape(R, M)
     acc_i[...] += dot_t(m_inner, u)
     acc_o[...] += dot_t(m_outer, u)
 
@@ -399,7 +419,7 @@
     def _():
         for i in range(GROUP):
             remote(u_send, uo_recv.at[i], ao_s.at[0], ao_r.at[i], {"sub": beyond, "blk": y}).wait_recv()
-        acc_o[...] += dot_t(mo_recv[...], uo_recv[...].reshape(R, M))
+        acc_o[...] += dot_t(mo_recv[...], unpack(uo_recv[...]).reshape(R, M))
 
     @pl.when(edge)
     def _():
@@ -438,7 +458,8 @@
 def shards(residual, stiffness, pattern, neumann_inv, dirichlet_inv, basis, node_ops, root_inv):
     vm = pltpu.VMEM
     dma = pltpu.SemaphoreType.DMA
-    chunk = (CHUNK, M)
+    chunk = (CHUNK * 3 // 2, 128)
+    wide = (R // YS * 3 // 2, 128)
     hbm = pl.BlockSpec(memory_space=pl.ANY)
     out = pl.pallas_call(
         kernel,
@@ -448,8 +469,8 @@
         scratch_shapes=[
             vm((B, 2, 2, 128), F32), vm((B, 2, B), BF), vm((2, M, B), BF), vm((6, M, M), F32), vm((M, M), F32),
             vm((2, B, R), BF), vm((2, B, R), F32), vm((2, B, M), BF), vm((2, B, M), F32),
-            vm((GROUP, *chunk), BF), vm((GROUP, *chunk), BF), vm((YS, R // YS, M), F32), vm((YS, R // YS, M), BF), vm((YS, R // YS, M), BF),
-            vm((R // YS, M), BF), vm((YS, R // YS, M), BF),
+            vm((GROUP, *chunk), BF), vm((GROUP, *chunk), BF), vm((YS, *wide), F32), vm((YS, *wide), BF), vm((YS, *wide), BF),
+            vm(wide, BF), vm((YS, *wide), BF),
             vm(chunk, BF), vm((ZS, *chunk), BF), vm(chunk, BF), vm((4, *chunk), BF), vm(chunk, BF), vm(chunk, BF),
             vm(chunk, BF), vm((XS, *chunk), BF), vm(chunk, BF), vm(chunk, BF), vm(chunk, BF), vm((GROUP, *chunk), BF),
             vm((GROUP, *chunk), BF),

time: 34.6 us -> 33.6 us (0.971)
  Pallas kernels: 33.6 us -> 32.7 us
    pallas_call x1, Pallas kernels: 33.6 us -> 32.7 us  [shards(): pl.pallas_call(kernel, out_shape=jax.ShapeDtypeStruct((B, 2, 2, 128), F32...]
where the time goes in v5:
time: 33.6 us
  Pallas kernels  32.7 us (97%)
  local copies, waits for them, and re-layouts  0.88 us (3%)
    pallas_call x1, Pallas kernels, shards(): pl.pallas_call(kernel, out_shape=jax.ShapeDtypeStruct((B, 2, 2, 128), F32...  32.7 us
    unnamed x1, local copies, waits for them, and re-layouts  0.88 us

profile of v5, /device:TPU:24, one launch (start us, length us, event | category | flops | bytes accessed | tf_op | source)
XLA Modules:
  0.0 33.6 jit_solution(6590882176866457254)
XLA Ops:
  0.0 32.7 %shard_map.82 = f32[375,2,2,128]{3,2,1,0:T(2,128)S(1)} custom-call(s32[2,16]{1,0:T(2,128)} %bitcast.27, f32[375,2,2,128]{3,2,1,0:T(2,128)} %bitcast.23, bf16[2,375,16,375]{3,2,1,0:T(8,128)(2,1)} %bitcast.21, bf16[375,2,375]{2,1,0:T(2,128)(2,1)} %bitcast.24, bf16[375,2,375]{2,1,0:T(2,128)(2,1)} %bitcast.25, bf16[2,192,375]{2,1,0:T(8,128)(2,1)} %bitcast.26, ...), custom_call_target="tpu_custom_call" | custom-call | tf_op jit(solution)/shard_map/pallas_call | solution.py:464
  32.7 0.9 %copy.10 = f32[1,2,375,256]{3,1,2,0:T(2,128)} copy(f32[1,2,375,256]{3,1,2,0:T(2,128)S(1)} %bitcast.20) | data formatting | bytes 1536000

commit v6 on v5

--- a/solution.py
+++ b/solution.py
@@ -102,6 +102,9 @@
             src_ref=src, dst_ref=dst, send_sem=ssem, recv_sem=rsem, device_id=peer, device_id_type=MESH
         )
 
+    def all_of(buffer, n, ssem, rsem):
+        return remote(buffer.at[0:n], buffer.at[0:n], ssem, rsem, group_peer(1))
+
     def send(*a):
         copy = remote(*a)
         copy.start()
@@ -127,7 +130,7 @@
 
     def ring(terms, ssem, rsem):
         def hop(slot, i, peer):
-            return remote(terms.at[slot], terms.at[slot], ssem.at[i], rsem.at[slot], peer)
+            return remote(terms.at[slot], terms.at[slot], ssem, rsem.at[slot], peer)
 
         return [
             hop(my_outer, 0, after), hop(my_outer, 1, before), hop(my_inner, 2, after), hop(my_inner, 3, before),
@@ -184,9 +187,9 @@
     rs = []
     for e in (4, 5, 2, 3, 6, 7, 1):
         target = flip(y, e >> 1) * 2 + flip(core, e & 1)
-        rs.append(send(rs_send.at[target], rs_recv.at[e], rs_s.at[e], rs_r.at[e], group_peer(e)))
+        rs.append(send(rs_send.at[target], rs_recv.at[e], rs_s, rs_r, group_peer(e)))
     ps = [
-        send(p_send.at[flip(y, e)], p_recv.at[e], ps_s.at[e], ps_r.at[e], {"sub": s, "blk": flip(y, e)}) for e in (2, 1, 3)
+        send(p_send.at[flip(y, e)], p_recv.at[e], ps_s, ps_r, {"sub": s, "blk": flip(y, e)}) for e in (2, 1, 3)
     ]
 
     n0h, n0l = split(n0)
@@ -228,7 +231,7 @@
         m_ring[3].start()
 
     def arrived(terms, ssem, rsem, slot):
-        remote(terms.at[slot], terms.at[slot], ssem.at[0], rsem.at[slot], after).wait_recv()
+        remote(terms.at[slot], terms.at[slot], ssem, rsem.at[slot], after).wait_recv()
 
     def mixing(n, padded):
         row = lax.broadcasted_iota(jnp.int32, (8 * padded, 16 * n), 0)
@@ -254,8 +257,7 @@
         mix_tail[...] = mixing(B % 16, 8)
         mix_rows(0, 192)
 
-    for c in rs:
-        c.wait_recv()
+    all_of(rs_recv, GROUP - 1, rs_s, rs_r).wait_recv()
     q1 = rs_send[me8].astype(F32)
     for e in range(1, GROUP):
         q1 = q1 + rs_recv[e].astype(F32)
@@ -264,18 +266,17 @@
     w3 = mm(q1, n123)
     w3 = pack(w3)
     w3_send[...] = w3.astype(BF)
-    zc = [send(w3_send, z_recv.at[d], z_s.at[d], z_r.at[d], z_peer(d)) for d in (4, 3, 5, 2, 6, 1, 7)]
-    for c in ps:
-        c.wait_recv()
+    zc = [send(w3_send, z_recv.at[d], z_s, z_r, z_peer(d)) for d in (4, 3, 5, 2, 6, 1, 7)]
+    all_of(p_recv, YS - 1, ps_s, ps_r).wait_recv()
     own_q0 = p_own[y] + (p_recv[1].astype(F32) + p_recv[2].astype(F32) + p_recv[3].astype(F32))
     q0_send[...] = own_q0.astype(BF)
-    qs = [send(q0_send, q0_recv.at[y], q0_s.at[e], q0_r.at[e], {"sub": s, "blk": flip(y, e)}) for e in (2, 1, 3)]
+    qs = [send(q0_send, q0_recv.at[y], q0_s, q0_r, {"sub": s, "blk": flip(y, e)}) for e in (2, 1, 3)]
     q0_recv[y] = own_q0.astype(BF)
 
     w2 = mm(q1, n12)
     w2 = pack(w2)
     w2_send[...] = w2.astype(BF)
-    q3c = [send(w2_send, q3_recv.at[d], q3_s.at[d], q3_r.at[d], z_peer(d)) for d in (1, 2, 3)]
+    q3c = [send(w2_send, q3_recv.at[d], q3_s, q3_r, z_peer(d)) for d in (1, 2, 3)]
     w1 = mm(q1, n1)
     w1 = pack(w1)
     w1_send[...] = w1.astype(BF)
@@ -293,8 +294,7 @@
     n45 = mm(n4, n5)
     t4 = mm(n123, n4)
     tr = mm(mm(t4, n5), root[...])
-    for c in qs:
-        c.wait_recv()
+    all_of(q0_recv, YS - 1, q0_s, q0_r).wait_recv()
     q0 = unpack(q0_recv[...]).reshape(R, M)
     for j in range(2):
         t = (fixed[j] + dot_t(bt[j], q0)) * scales[j]
@@ -316,8 +316,7 @@
         t_ring[2].start()
         t_ring[3].start()
 
-    for c in zc:
-        c.wait_recv()
+    all_of(z_recv, ZS - 1, z_s, z_r).wait_recv()
     q4 = w3
     for d in range(1, ZS):
         q4 = q4 + z_recv[d].astype(F32)
@@ -325,7 +324,7 @@
     v5 = mm(q4, n45)
     v5 = pack(v5)
     v5_send[...] = v5.astype(BF)
-    xc = [send(v5_send, x_recv.at[d], x_s.at[d], x_r.at[d], x_peer(d)) for d in (2, 1, 3)]
+    xc = [send(v5_send, x_recv.at[d], x_s, x_r, x_peer(d)) for d in (2, 1, 3)]
     v4 = mm(q4, n4)
     v4 = pack(v4)
     v4_send[...] = v4.astype(BF)
@@ -335,7 +334,8 @@
     def _():
         to.start()
 
-    for c in q3c + q2c:
+    all_of(q3_recv, 3, q3_s, q3_r).wait_recv()
+    for c in q2c:
         c.wait_recv()
     q3 = unpack(w2 + (q3_recv[1].astype(F32) + q3_recv[2].astype(F32) + q3_recv[3].astype(F32)))
     q2 = unpack(w1 + q2_recv[...].astype(F32))
@@ -364,15 +364,16 @@
     def _():
         dir_b[...] = dir_v[:, 1, :]
 
-    for c in xc + q5c:
+    all_of(x_recv, XS - 1, x_s, x_r).wait_recv()
+    for c in q5c:
         c.wait_recv()
     q6 = unpack(v5 + (x_recv[1].astype(F32) + x_recv[2].astype(F32) + x_recv[3].astype(F32)))
     q5 = unpack(v4 + q5_recv[...].astype(F32))
     u1 = mm_t(q6, tr) + mm_t(q5, t4) + rest
     u_send[...] = pack(u1).astype(BF)
-    ag = [send(u_send, u_recv.at[me8], ag_s.at[e], ag_r.at[e], group_peer(e)) for e in (4, 5, 2, 3, 6, 7, 1)]
-    above = [remote(u_send, uo_recv.at[me8], ao_s.at[e], ao_r.at[me8], {"sub": up, "blk": flip(y, e)}) for e in range(YS)]
-    below = [remote(u_send, uo_recv.at[me8], ao_s.at[4 + e], ao_r.at[me8], {"sub": down, "blk": flip(y, e)}) for e in range(YS)]
+    ag = [send(u_send, u_recv.at[me8], ag_s, ag_r, group_peer(e)) for e in (4, 5, 2, 3, 6, 7, 1)]
+    above = [remote(u_send, uo_recv.at[me8], ao_s.at[0], ao_r, {"sub": up, "blk": flip(y, e)}) for e in range(YS)]
+    below = [remote(u_send, uo_recv.at[me8], ao_s.at[1], ao_r, {"sub": down, "blk": flip(y, e)}) for e in range(YS)]
 
     @pl.when(has_up)
     def _():
@@ -390,14 +391,14 @@
     def _():
         arrived(et, et_s, et_r, from_before)
         t_ring[4].start()
+        arrived(et, et_s, et_r, from_after)
+        t_ring[5].start()
         for slot in far:
             arrived(em, em_s, em_r, slot)
         total = dot(sums[my_outer], em[my_outer])
         for slot in near[1:] + far:
             total = total + dot(sums[slot], em[slot])
         mixed[...] = total.astype(BF)
-        arrived(et, et_s, et_r, from_after)
-        t_ring[5].start()
         total = dot(sums[my_outer], et[my_outer])
         for slot in near[1:]:
             total = total + dot(sums[slot], et[slot])
@@ -409,16 +410,14 @@
         acc_o[...] += to_recv[...].astype(F32)
         mo.wait_recv()
 
-    for c in ag:
-        c.wait_recv()
+    all_of(u_recv, GROUP - 1, ag_s, ag_r).wait_recv()
     u = unpack(u_recv[...]).reshape(R, M)
     acc_i[...] += dot_t(m_inner, u)
     acc_o[...] += dot_t(m_outer, u)
 
     @pl.when(has_outer)
     def _():
-        for i in range(GROUP):
-            remote(u_send, uo_recv.at[i], ao_s.at[0], ao_r.at[i], {"sub": beyond, "blk": y}).wait_recv()
+        all_of(uo_recv, GROUP, ao_s.at[0], ao_r).wait_recv()
         acc_o[...] += dot_t(mo_recv[...], unpack(uo_recv[...]).reshape(R, M))
 
     @pl.when(edge)
@@ -428,15 +427,22 @@
             terms[...] += dot(sums[slot], et[slot])
         coupled = terms[...] + dot_t(mixed[...], u)
         acc_o[...] -= dot(dir_b[...], coupled.astype(BF))
-        for c in m_ring + t_ring:
-            c.wait_send()
+        all_of(em, 6, em_s, em_r.at[0]).wait_send()
+        all_of(et, 6, et_s, et_r.at[0]).wait_send()
 
     for h in range(2):
         a, b = acc_o[:, h * 128 : (h + 1) * 128], acc_i[:, h * 128 : (h + 1) * 128]
         out[:, h, 0, :] = jnp.where(core == 0, a, b)
         out[:, h, 1, :] = jnp.where(core == 0, b, a)
 
-    for c in rs + ps + qs + zc + q3c + q2c + xc + q5c + ag + [mi, ti]:
+    all_of(rs_recv, GROUP - 1, rs_s, rs_r).wait_send()
+    all_of(p_recv, YS - 1, ps_s, ps_r).wait_send()
+    all_of(q0_recv, YS - 1, q0_s, q0_r).wait_send()
+    all_of(z_recv, ZS - 1, z_s, z_r).wait_send()
+    all_of(q3_recv, 3, q3_s, q3_r).wait_send()
+    all_of(x_recv, XS - 1, x_s, x_r).wait_send()
+    all_of(u_recv, GROUP - 1, ag_s, ag_r).wait_send()
+    for c in q2c + q5c + [mi, ti]:
         c.wait_send()
 
     @pl.when(has_outer)
@@ -446,13 +452,11 @@
 
     @pl.when(has_up)
     def _():
-        for c in above:
-            c.wait_send()
+        all_of(uo_recv, YS, ao_s.at[0], ao_r).wait_send()
 
     @pl.when(has_down)
     def _():
-        for c in below:
-            c.wait_send()
+        all_of(uo_recv, YS, ao_s.at[1], ao_r).wait_send()
 
 
 def shards(residual, stiffness, pattern, neumann_inv, dirichlet_inv, basis, node_ops, root_inv):
@@ -478,9 +482,8 @@
             vm((B, R), F32), vm((B, R), F32),
             vm((B, 16, B), BF), vm((8, B, B), BF), vm((B, 2, B), BF), vm((B, B), BF), vm((B, M), BF), vm((B, R), F32),
             vm((8, B, M), BF), vm((8, B, R), BF), vm((2, 16), jnp.int32), vm((128, 256), BF), vm((64, 112), BF),
-            dma((8,)), dma((8,)), dma((8,)), dma((4,)), dma((4,)), dma((4,)), dma((4,)), dma((8,)), dma((8,)), dma((4,)), dma((4,)),
-            dma(()), dma(()), dma((4,)), dma((4,)), dma(()), dma(()), dma((8,)), dma((8,)), dma((8,)), dma((8,)),
-            dma((4,)), dma((4,)), dma((6,)), dma((8,)), dma((6,)), dma((8,)),
+            dma((8,)), *[dma(())] * 18, dma((2,)), dma(()),
+            dma((4,)), dma((4,)), dma(()), dma((8,)), dma(()), dma((8,)),
         ],
         compiler_params=pltpu.CompilerParams(collective_id=0, has_side_effects=True, vmem_limit_bytes=48 << 20),
     )(

time: 33.6 us -> 32.8 us (0.976)
  Pallas kernels: 32.7 us -> 31.8 us
    pallas_call x1, Pallas kernels: 32.7 us -> 31.8 us  [shards(): pl.pallas_call(kernel, out_shape=jax.ShapeDtypeStruct((B, 2, 2, 128), F32...]
where the time goes in v6:
time: 32.8 us; the launch traced here: 32.7 us
  Pallas kernels  31.8 us (97%)
  local copies, waits for them, and re-layouts  0.88 us (3%)
    pallas_call x1, Pallas kernels, shards(): pl.pallas_call(kernel, out_shape=jax.ShapeDtypeStruct((B, 2, 2, 128), F32...  31.8 us
    unnamed x1, local copies, waits for them, and re-layouts  0.88 us

profile of v6, /device:TPU:24, one launch (start us, length us, event | category | flops | bytes accessed | tf_op | source)
XLA Modules:
  0.0 32.7 jit_solution(14349776398135840763)
XLA Ops:
  0.0 31.8 %shard_map.82 = f32[375,2,2,128]{3,2,1,0:T(2,128)S(1)} custom-call(s32[2,16]{1,0:T(2,128)} %bitcast.27, f32[375,2,2,128]{3,2,1,0:T(2,128)} %bitcast.23, bf16[2,375,16,375]{3,2,1,0:T(8,128)(2,1)} %bitcast.21, bf16[375,2,375]{2,1,0:T(2,128)(2,1)} %bitcast.24, bf16[375,2,375]{2,1,0:T(2,128)(2,1)} %bitcast.25, bf16[2,192,375]{2,1,0:T(8,128)(2,1)} %bitcast.26, ...), custom_call_target="tpu_custom_call" | custom-call | tf_op jit(solution)/shard_map/pallas_call | solution.py:468
  31.8 0.9 %copy.10 = f32[1,2,375,256]{3,1,2,0:T(2,128)} copy(f32[1,2,375,256]{3,1,2,0:T(2,128)S(1)} %bitcast.20) | data formatting | bytes 1536000

commit v7 on v6

--- a/solution.py
+++ b/solution.py
@@ -137,7 +137,14 @@
             hop(from_before, 4, after), hop(from_after, 5, before),
         ]
 
-    m_ring, t_ring = ring(em, em_s, em_r), ring(et, et_s, et_r)
+    t_ring = ring(et, et_s, et_r)
+    m_ring = [
+        remote(em.at[slot], em.at[slot], em_s, em_r.at[k], peer)
+        for slot, k, peer in (
+            (my_outer, 0, after), (my_outer, 2, before), (my_inner, 2, after), (my_inner, 1, before),
+            (from_before, 2, after), (from_after, 2, before),
+        )
+    ]
 
     barrier = pltpu.get_barrier_semaphore()
 
@@ -284,9 +291,9 @@
 
     @pl.when(edge)
     def _():
-        arrived(em, em_s, em_r, from_before)
+        remote(em.at[from_before], em.at[from_before], em_s, em_r.at[0], after).wait_recv()
         m_ring[4].start()
-        arrived(em, em_s, em_r, from_after)
+        remote(em.at[from_after], em.at[from_after], em_s, em_r.at[1], after).wait_recv()
         m_ring[5].start()
         mix_rows(192, B)
 
@@ -393,8 +400,7 @@
         t_ring[4].start()
         arrived(et, et_s, et_r, from_after)
         t_ring[5].start()
-        for slot in far:
-            arrived(em, em_s, em_r, slot)
+        all_of(em, 4, em_s, em_r.at[2]).wait_recv()
         total = dot(sums[my_outer], em[my_outer])
         for slot in near[1:] + far:
             total = total + dot(sums[slot], em[slot])
@@ -483,7 +489,7 @@
             vm((B, 16, B), BF), vm((8, B, B), BF), vm((B, 2, B), BF), vm((B, B), BF), vm((B, M), BF), vm((B, R), F32),
             vm((8, B, M), BF), vm((8, B, R), BF), vm((2, 16), jnp.int32), vm((128, 256), BF), vm((64, 112), BF),
             dma((8,)), *[dma(())] * 18, dma((2,)), dma(()),
-            dma((4,)), dma((4,)), dma(()), dma((8,)), dma(()), dma((8,)),
+            dma((4,)), dma((4,)), dma(()), dma((3,)), dma(()), dma((8,)),
         ],
         compiler_params=pltpu.CompilerParams(collective_id=0, has_side_effects=True, vmem_limit_bytes=48 << 20),
     )(

time: 32.8 us -> 32.7 us (level)
  no operation moved by 1% of the time
where the time goes in v7:
time: 32.7 us
  Pallas kernels  31.8 us (97%)
  local copies, waits for them, and re-layouts  0.88 us (3%)
    pallas_call x1, Pallas kernels, shards(): pl.pallas_call(kernel, out_shape=jax.ShapeDtypeStruct((B, 2, 2, 128), F32...  31.8 us
    unnamed x1, local copies, waits for them, and re-layouts  0.88 us

profile of v7, /device:TPU:24, one launch (start us, length us, event | category | flops | bytes accessed | tf_op | source)
XLA Modules:
  0.0 32.7 jit_solution(8000352977272338799)
XLA Ops:
  0.0 31.8 %shard_map.82 = f32[375,2,2,128]{3,2,1,0:T(2,128)S(1)} custom-call(s32[2,16]{1,0:T(2,128)} %bitcast.27, f32[375,2,2,128]{3,2,1,0:T(2,128)} %bitcast.23, bf16[2,375,16,375]{3,2,1,0:T(8,128)(2,1)} %bitcast.21, bf16[375,2,375]{2,1,0:T(2,128)(2,1)} %bitcast.24, bf16[375,2,375]{2,1,0:T(2,128)(2,1)} %bitcast.25, bf16[2,192,375]{2,1,0:T(8,128)(2,1)} %bitcast.26, ...), custom_call_target="tpu_custom_call" | custom-call | tf_op jit(solution)/shard_map/pallas_call | solution.py:474
  31.8 0.9 %copy.10 = f32[1,2,375,256]{3,1,2,0:T(2,128)} copy(f32[1,2,375,256]{3,1,2,0:T(2,128)S(1)} %bitcast.20) | data formatting | bytes 1536000
